TPU v7x, 512 devices: a whole 4x4x16 slice. The times are simulated.
512 devices in a mesh: grp: 16 (over z), tile: 32 (over x, y, core).
Axes of the slice: x: 4, y: 4, z: 16, core: 2. Of those that a mesh axis runs over, the one named last changes fastest.
Arguments:
- seg_stream: int32 [512, 512, 32], P(('grp', 'tile')), may hold values from 0 to 1023
- seg_voxel: int32 [512, 512, 32], P(('grp', 'tile')), may hold values from 0 to 127
- seg_bin: int32 [512, 512, 32], P(('grp', 'tile')), may hold values from 0 to 511
- seg_length: float32 [512, 512, 32], P(('grp', 'tile')), may hold values from 0.02 to 0.06
- seg_count: int32 [512, 512], P(('grp', 'tile')), may hold values from 6 to 32, as said below
- stream_weight: float32 [524288], P(('grp', 'tile')), may hold values from 0 to 2
- signal: bfloat16 [288, 65536], P(None, ('grp', 'tile')), may hold values from 0.19921875 to 2
- peak_bin: int32 [3, 65536], P(None, ('grp', 'tile')), may hold values from 0 to 511
- extra_weight: float32 [3, 65536], P(None, ('grp', 'tile')), may hold values from 0 to 1
- iso_weight: float32 [65536], P(('grp', 'tile')), may hold values from 0 to 1
- intra_kernel: float32 [288, 512], replicated, may hold values from 0 to 1
- extra_kernel: float32 [288, 512], replicated, may hold values from 0 to 1
- iso_kernel: float32 [288], replicated, may hold values from 0.3 to 1
- step_size: float32 [1], replicated, may hold values from 0.0010416667 to 0.004166667
Outputs:
- residual: float32 [288, 65536], P(None, ('grp', 'tile'))
- new_stream: float32 [524288], P(('grp', 'tile'))
- new_extra: float32 [3, 65536], P(None, ('grp', 'tile'))
- new_iso: float32 [65536], P(('grp', 'tile'))
Inputs may be any that keep to these rules, and one draw needn't show every extreme that they name: `seg_count`: some tile receives 32 used slots from every streamline owner.
All inputs are finite; a program needn't handle non-finite values.
Results may differ from a plain program's by a relative error of at most 0.0003.
Values sent between devices are 32-bit elements; how exact they have to be, the bound alone decides.
No kernel may reach another device: no remote copies, remote signals or barrier semaphores. Data moves between devices by JAX's collectives and lax.ppermute only.
A program may use at most 64 MiB of HBM per device.

v0:
```python
import jax
import jax.numpy as jnp
from jax import lax
from jax.sharding import PartitionSpec as P


def send_forward(outgoing):
    return (
        lax.all_to_all(
            lax.all_to_all(outgoing[0], "grp", split_axis=0, concat_axis=0, tiled=True),
            "tile",
            split_axis=1,
            concat_axis=1,
            tiled=True,
        ),
        lax.all_to_all(
            lax.all_to_all(outgoing[1], "grp", split_axis=0, concat_axis=0, tiled=True),
            "tile",
            split_axis=1,
            concat_axis=1,
            tiled=True,
        ),
    )


def send_return(seg_back):
    return lax.all_to_all(
        lax.all_to_all(seg_back, "grp", split_axis=0, concat_axis=0, tiled=True),
        "tile",
        split_axis=1,
        concat_axis=1,
        tiled=True,
    )


def background_signal(peak_bin, extra_weight, iso_weight, extra_kernel, iso_kernel):
    num_bins = extra_kernel.shape[1]
    bin_ids = lax.broadcasted_iota(jnp.int32, (1, num_bins, 1), 1)
    extra_map = jnp.sum(
        jnp.where(peak_bin[:, None, :] == bin_ids, extra_weight[:, None, :], 0.0), axis=0
    )
    zeppelin = jnp.dot(extra_kernel, extra_map, precision=lax.Precision.HIGHEST)
    return zeppelin + iso_kernel[:, None] * iso_weight[None, :]


def on_device(
    seg_stream,
    seg_voxel,
    seg_bin,
    seg_length,
    seg_count,
    stream_weight,
    signal,
    peak_bin,
    extra_weight,
    iso_weight,
    intra_kernel,
    extra_kernel,
    iso_kernel,
    step_size,
):
    high = lax.Precision.HIGHEST
    group_count = lax.axis_size("grp")
    tile_count = lax.axis_size("tile")
    owner_count = group_count * tile_count
    block_size = seg_stream.shape[2]
    num_bins = intra_kernel.shape[1]
    num_voxels = signal.shape[1]
    slot_index = lax.broadcasted_iota(jnp.int32, (owner_count, block_size), 1)
    live_mask = (slot_index < seg_count[0][:, None]).astype(jnp.float32)
    length_live = seg_length[0] * live_mask
    seg_value = jnp.take(stream_weight, seg_stream[0], axis=0) * length_live
    seg_keys = seg_bin[0] * num_voxels + seg_voxel[0]
    outgoing = (
        seg_value.reshape(group_count, tile_count, block_size),
        seg_keys.reshape(group_count, tile_count, block_size),
    )
    arrived_value, arrived_keys = send_forward(outgoing)
    backdrop = background_signal(peak_bin, extra_weight, iso_weight, extra_kernel, iso_kernel)
    flat_keys = arrived_keys.reshape(-1)
    fiber_map = jax.ops.segment_sum(
        arrived_value.reshape(-1), flat_keys, num_segments=num_bins * num_voxels
    ).reshape(num_bins, num_voxels)
    residual = (
        jnp.dot(intra_kernel, fiber_map, precision=high) + backdrop - signal.astype(jnp.float32)
    )
    contract = (((0,), (0,)), ((), ()))
    intra_back = lax.dot_general(intra_kernel, residual, contract, precision=high)
    extra_back = lax.dot_general(extra_kernel, residual, contract, precision=high)
    seg_back = jnp.take(intra_back.reshape(-1), flat_keys).reshape(arrived_keys.shape)
    returned = send_return(seg_back)
    contrib = returned.reshape(owner_count, block_size) * length_live
    stream_grad = jax.ops.segment_sum(
        contrib.reshape(-1), seg_stream[0].reshape(-1), num_segments=stream_weight.shape[0]
    )
    step = step_size[0]
    new_stream = jnp.maximum(stream_weight - step * stream_grad, 0.0)
    extra_grad = jnp.take_along_axis(extra_back, peak_bin, axis=0)
    new_extra = jnp.maximum(extra_weight - step * extra_grad, 0.0)
    iso_grad = jnp.dot(iso_kernel, residual, precision=high)
    new_iso = jnp.maximum(iso_weight - step * iso_grad, 0.0)
    return (residual, new_stream, new_extra, new_iso)


def solution(mesh):
    return jax.shard_map(
        on_device,
        mesh=mesh,
        in_specs=(
            P(("grp", "tile"), None, None),
            P(("grp", "tile"), None, None),
            P(("grp", "tile"), None, None),
            P(("grp", "tile"), None, None),
            P(("grp", "tile"), None),
            P(("grp", "tile")),
            P(None, ("grp", "tile")),
            P(None, ("grp", "tile")),
            P(None, ("grp", "tile")),
            P(("grp", "tile")),
            P(),
            P(),
            P(),
            P(),
        ),
        out_specs=(
            P(None, ("grp", "tile")),
            P(("grp", "tile")),
            P(None, ("grp", "tile")),
            P(("grp", "tile")),
        ),
        check_vma=False,
    )
```

profile of v0, /device:TPU:1, one launch (start us, length us, event | category | flops | bytes accessed | tf_op | source)
XLA Modules:
  0.0 465.9 jit_solution(18097590152550445483)
XLA Ops:
  0.6 0.9 multiply_add_fusion
  2.6 15.9 %all-to-all-start = ((s32[16,1,1024]{2,1,0:T(1,128)}), s32[16,1,1024]{2,1,0:T(1,128)S(1)}, u32[]{:S(2)}, u32[]{:S(2)}) async-start(s32[16,1,1024]{2,1,0:T(1,128)} %reshape.194), calls=%async_computation | async-start | bytes 131072 | tf_op jit(solution)/shard_map/all_to_all | solution.py:17
  20.9 65.3 %gather_fusion = f32[16384]{0:T(1024)S(1)} fusion(f32[1024]{0:T(1024)S(1)} %copy-done.1, s32[16384]{0:T(1024)S(1)} %broadcast_clamp_fusion.1), kind=kCustom, calls=%fused_computation | custom fusion | bytes 196608 | tf_op jit(solution)/shard_map/jit(_take)/gather | solution.py:72
  88.9 11.5 %all-to-all-start.2 = ((f32[16,1,1024]{2,1,0:T(1,128)}), f32[16,1,1024]{2,1,0:T(1,128)S(1)}, u32[]{:S(2)}, u32[]{:S(2)}) async-start(f32[16,1,1024]{2,1,0:T(1,128)} %reshape.198), calls=%async_computation.2 | async-start | bytes 131072 | tf_op jit(solution)/shard_map/all_to_all | solution.py:10
  101.5 0.8 reduce.4
  102.6 0.8 reshape.196
  103.4 8.6 %all-to-all-done.2 = f32[16,1,1024]{2,1,0:T(1,128)S(1)} async-done(((f32[16,1,1024]{2,1,0:T(1,128)}), f32[16,1,1024]{2,1,0:T(1,128)S(1)}, u32[]{:S(2)}, u32[]{:S(2)}) %all-to-all-start.2) | async-done | bytes 65568 | tf_op jit(solution)/shard_map/all_to_all | solution.py:10
  112.0 9.8 %all-to-all-start.1 = ((s32[32,1,512]{2,1,0:T(1,128)}), s32[32,1,512]{2,1,0:T(1,128)S(1)}, u32[]{:S(2)}, u32[]{:S(2)}) async-start(s32[32,1,512]{2,1,0:T(1,128)} %reshape.196), calls=%async_computation.1 | async-start | bytes 131072 | tf_op jit(solution)/shard_map/all_to_all | solution.py:16
  123.4 0.8 reduce.6
  125.3 3.9 all-to-all-done.1
  129.2 3.9 all-to-all-start.3
  133.1 0.8 reduce.5
  134.5 6.1 %all-to-all-done.3 = f32[32,1,512]{2,1,0:T(1,128)S(1)} async-done(((f32[32,1,512]{2,1,0:T(1,128)}), f32[32,1,512]{2,1,0:T(1,128)S(1)}, u32[]{:S(2)}, u32[]{:S(2)}) %all-to-all-start.3) | async-done | bytes 65568 | tf_op jit(solution)/shard_map/all_to_all | solution.py:9
  140.6 0.8 reduce.7
  141.7 85.9 %scatter_custom_fusion = f32[65536]{0:T(1024)S(1)} fusion(s32[16384]{0:T(1024)S(1)} %reshape.156, f32[16384]{0:T(1024)S(1)} %reshape.158, f32[]{:T(128)} %constant.31.clone.1), kind=kCustom, calls=%fused_computation.27 | custom fusion | flops 16384 | bytes 262148 | tf_op jit(solution)/shard_map/scatter-add | solution.py:81
  229.1 90.5 %gather_fusion.1 = f32[16384]{0:T(1024)S(1)} fusion(f32[65536]{0:T(1024)S(1)} %bitcast.77, s32[16384]{0:T(1024)S(1)} %broadcast_clamp_fusion), kind=kCustom, calls=%fused_computation.1 | custom fusion | bytes 196608 | tf_op jit(solution)/shard_map/jit(_take)/gather | solution.py:90
  320.7 3.5 all-to-all-start.4
  324.9 3.5 gather_fusion.2
  329.1 6.8 %all-to-all-done.4 = f32[16,1,1024]{2,1,0:T(1,128)S(1)} async-done(((f32[16,1,1024]{2,1,0:T(1,128)}), f32[16,1,1024]{2,1,0:T(1,128)S(1)}, u32[]{:S(2)}, u32[]{:S(2)}) %all-to-all-start.4) | async-done | bytes 65568 | tf_op jit(solution)/shard_map/all_to_all | solution.py:28
  335.9 0.8 reduce.8
  337.7 5.5 %all-to-all-start.5 = ((f32[32,1,512]{2,1,0:T(1,128)}), f32[32,1,512]{2,1,0:T(1,128)S(1)}, u32[]{:S(2)}, u32[]{:S(2)}) async-start(f32[32,1,512]{2,1,0:T(1,128)} %reshape.204), calls=%async_computation.5 | async-start | bytes 131072 | tf_op jit(solution)/shard_map/all_to_all | solution.py:27
  343.9 6.9 %all-to-all-done.5 = f32[32,1,512]{2,1,0:T(1,128)S(1)} async-done(((f32[32,1,512]{2,1,0:T(1,128)}), f32[32,1,512]{2,1,0:T(1,128)S(1)}, u32[]{:S(2)}, u32[]{:S(2)}) %all-to-all-start.5) | async-done | bytes 65568 | tf_op jit(solution)/shard_map/all_to_all | solution.py:27
  350.7 0.8 reduce.9
  351.9 113.4 %scatter_custom_fusion.1 = f32[1024]{0:T(1024)S(1)} fusion(s32[16384]{0:T(1024)S(1)} %reshape.164, f32[16384]{0:T(1024)S(1)} %select_multiply_fusion.1, f32[]{:T(128)} %constant.31.clone.1), kind=kCustom, calls=%fused_computation.41 | custom fusion | flops 16384 | bytes 4100 | tf_op jit(solution)/shard_map/scatter-add | solution.py:93
  (81 shorter events, 16.6 us)
Async XLA Ops:
  0.6 227.0 %copy-start = (f32[288,512]{1,0:T(8,128)S(1)}, f32[288,512]{1,0:T(8,128)}, u32[]{:S(2)}) copy-start(f32[288,512]{1,0:T(8,128)} %param.24) | copy-start | bytes 1769476
  2.6 15.9 %copy-start.4 = (s32[1,512,32]{1,2,0:T(8,128)S(1)}, s32[1,512,32]{1,2,0:T(8,128)}, u32[]{:S(2)}) copy-start(s32[1,512,32]{1,2,0:T(8,128)} %param.14) | copy-start | bytes 196612
  2.6 86.3 %all-to-all-start = ((s32[16,1,1024]{2,1,0:T(1,128)}), s32[16,1,1024]{2,1,0:T(1,128)S(1)}, u32[]{:S(2)}, u32[]{:S(2)}) async-start(s32[16,1,1024]{2,1,0:T(1,128)} %reshape.194), calls=%async_computation | async-start | bytes 131072 | tf_op jit(solution)/shard_map/all_to_all | solution.py:17
  18.5 0.7 copy-start.10
  20.2 0.7 copy-start.1
  86.2 0.8 copy-start.6
  87.1 0.7 copy-start.7
  87.1 0.7 copy-start.8
  87.8 12.5 %copy-start.3 = (f32[288,512]{1,0:T(8,128)S(1)}, f32[288,512]{1,0:T(8,128)}, u32[]{:S(2)}) copy-start(f32[288,512]{1,0:T(8,128)} %param.25) | copy-start | bytes 1769476
  88.8 11.5 %copy-start.9 = (f32[288]{0:T(512)S(1)}, f32[288]{0:T(512)}, u32[]{:S(2)}) copy-start(f32[288]{0:T(512)} %param.26) | copy-start | bytes 3460
  88.8 11.5 %copy-start.11 = (f32[128]{0:T(128)S(1)}, f32[128]{0:T(128)}, u32[]{:S(2)}) copy-start(f32[128]{0:T(128)} %param.23) | copy-start | bytes 1540
  88.9 23.2 %all-to-all-start.2 = ((f32[16,1,1024]{2,1,0:T(1,128)}), f32[16,1,1024]{2,1,0:T(1,128)S(1)}, u32[]{:S(2)}, u32[]{:S(2)}) async-start(f32[16,1,1024]{2,1,0:T(1,128)} %reshape.198), calls=%async_computation.2 | async-start | bytes 131072 | tf_op jit(solution)/shard_map/all_to_all | solution.py:10
  112.0 17.2 %all-to-all-start.1 = ((s32[32,1,512]{2,1,0:T(1,128)}), s32[32,1,512]{2,1,0:T(1,128)S(1)}, u32[]{:S(2)}, u32[]{:S(2)}) async-start(s32[32,1,512]{2,1,0:T(1,128)} %reshape.196), calls=%async_computation.1 | async-start | bytes 131072 | tf_op jit(solution)/shard_map/all_to_all | solution.py:16
  129.2 11.4 %all-to-all-start.3 = ((f32[32,1,512]{2,1,0:T(1,128)}), f32[32,1,512]{2,1,0:T(1,128)S(1)}, u32[]{:S(2)}, u32[]{:S(2)}) async-start(f32[32,1,512]{2,1,0:T(1,128)} %reshape.200), calls=%async_computation.3 | async-start | bytes 131072 | tf_op jit(solution)/shard_map/all_to_all | solution.py:9
  141.7 85.9 %copy-start.5 = (bf16[288,128]{1,0:T(8,128)(2,1)S(1)}, bf16[288,128]{1,0:T(8,128)(2,1)}, u32[]{:S(2)}) copy-start(bf16[288,128]{1,0:T(8,128)(2,1)} %param.20) | copy-start | bytes 221188
  228.3 100.0 %copy-start.2 = (f32[288,128]{1,0:T(8,128)}, f32[288,128]{1,0:T(8,128)S(1)}, u32[]{:S(2)}) copy-start(f32[288,128]{1,0:T(8,128)S(1)} %fusion.2) | copy-start | bytes 442372
  320.7 15.1 %all-to-all-start.4 = ((f32[16,1,1024]{2,1,0:T(1,128)}), f32[16,1,1024]{2,1,0:T(1,128)S(1)}, u32[]{:S(2)}, u32[]{:S(2)}) async-start(f32[16,1,1024]{2,1,0:T(1,128)} %reshape.202), calls=%async_computation.4 | async-start | bytes 131072 | tf_op jit(solution)/shard_map/all_to_all | solution.py:28
  337.7 13.0 %all-to-all-start.5 = ((f32[32,1,512]{2,1,0:T(1,128)}), f32[32,1,512]{2,1,0:T(1,128)S(1)}, u32[]{:S(2)}, u32[]{:S(2)}) async-start(f32[32,1,512]{2,1,0:T(1,128)} %reshape.204), calls=%async_computation.5 | async-start | bytes 131072 | tf_op jit(solution)/shard_map/all_to_all | solution.py:27
where the time goes:
time: 467 us; the launch traced here: 466 us
  other arithmetic  208 us (45%)
  local copies, waits for them, and re-layouts  171 us (37%)
  starting transfers between devices  50.1 us (11%)
  waiting for transfers between devices  32.3 us (7%)
    scatter-add x1, other arithmetic, on_device(): jax.ops.segment_sum(contrib.reshape(-1), seg_stream[0].reshape(-1), num_s...  113 us
    gather x2, local copies, waits for them, and re-layouts, on_device(): jnp.take(intra_back.reshape(-1), flat_keys).reshape(arrived_keys.shape)  90.7 us
    scatter-add x1, other arithmetic, on_device(): jax.ops.segment_sum(arrived_value.reshape(-1), flat_keys, num_segments=nu...  85.9 us
    gather x2, local copies, waits for them, and re-layouts, on_device(): seg_value = jnp.take(stream_weight, seg_stream[0], axis=0) * length_live  65.4 us
    all_to_all x1, starting transfers between devices, send_forward(): lax.all_to_all(outgoing[1], 'grp', split_axis=0, concat_axis=0, tiled=True)  15.9 us
    all_to_all x1, starting transfers between devices, send_forward(): lax.all_to_all(outgoing[0], 'grp', split_axis=0, concat_axis=0, tiled=True)  11.5 us
    all_to_all x1, starting transfers between devices, send_forward(): lax.all_to_all(lax.all_to_all(outgoing[1], 'grp', split_axis=0, concat_ax...  9.79 us
  transfers between devices with their start and end apart: 6, of which 5 were waited for; matrix products, arithmetic and copies ran while one was open for 17% of the time, Pallas kernels for 0%

commit v1 on v0

v1 whole, which is shorter than its diff:
```python
import jax
import jax.numpy as jnp
from jax import lax
from jax.experimental import pallas as pl
from jax.experimental.pallas import tpu as pltpu
from jax.sharding import PartitionSpec as P

LANES = 128
F32 = jnp.float32
BF16 = jnp.bfloat16
HIGH = lax.Precision.HIGHEST


def iota(shape, dim):
    return lax.broadcasted_iota(jnp.int32, shape, dim)


def split2(x):
    head = x.astype(BF16)
    return head, (x - head.astype(F32)).astype(BF16)


def dot(a, b, dims):
    return lax.dot_general(a, b, (dims, ((), ())), preferred_element_type=F32)


def pack_rows(ref, per_row, rows):
    parts = [ref[0, pl.ds(q, rows, stride=per_row), :] for q in range(per_row)]
    return jnp.concatenate(parts, axis=1)


def prepare_kernel(stream_ref, voxel_ref, bin_ref, length_ref, count_ref, weight_ref,
                   out_ref, stream_out_ref, length_out_ref, *, num_voxels):
    owners, block = stream_ref.shape[1], stream_ref.shape[2]
    per_row = LANES // block
    rows = owners // per_row
    groups = out_ref.shape[0]
    half = rows // groups
    picked = jnp.where(iota((rows, owners), 1) // per_row == iota((rows, owners), 0),
                       count_ref[...].astype(F32), 0.0).astype(BF16)
    spread = (iota((owners, LANES), 0) % per_row
              == iota((owners, LANES), 1) // block).astype(F32).astype(BF16)
    counts = dot(picked, spread, ((1,), (0,)))
    slot = (iota((rows, LANES), 1) % block).astype(F32)
    length = jnp.where(slot < counts, pack_rows(length_ref, per_row, rows), 0.0)
    stream = pack_rows(stream_ref, per_row, rows)
    keys = pack_rows(bin_ref, per_row, rows) * num_voxels + pack_rows(voxel_ref, per_row, rows)
    lane_id = stream % LANES
    row_id = stream // LANES
    weight = jnp.zeros((rows, LANES), F32)
    for r in range(weight_ref.shape[0]):
        table = jnp.broadcast_to(weight_ref[r:r + 1, :], (rows, LANES))
        found = jnp.take_along_axis(table, lane_id, axis=1)
        weight = jnp.where(row_id == r, found, weight)
    value = weight * length
    keys = keys.astype(F32)
    for g in range(groups):
        out_ref[g, :half, :] = value[g * half:(g + 1) * half, :]
        out_ref[g, half:, :] = keys[g * half:(g + 1) * half, :]
    stream_out_ref[...] = stream
    length_out_ref[...] = length


def regroup_kernel(in_ref, out_ref, *, block, arrays):
    groups = in_ref.shape[0]
    per_row = LANES // block
    tile_rows = in_ref.shape[1] // arrays
    group_rows = groups // per_row
    stride = per_row * arrays * group_rows
    lane_part = iota((tile_rows, LANES), 1) // block
    for k in range(arrays):
        for a in range(group_rows):
            x = [in_ref[a * per_row + b, k * tile_rows:(k + 1) * tile_rows, :] for b in range(per_row)]
            for q in range(per_row):
                y = None
                for b in range(per_row):
                    shift = (block * (b - q)) % LANES
                    moved = pltpu.roll(x[b], shift, axis=1) if shift else x[b]
                    y = moved if y is None else jnp.where(lane_part == b, moved, y)
                out_ref[pl.ds(q * arrays * group_rows + k * group_rows + a, tile_rows, stride=stride), :] = y


def ungroup_kernel(in_ref, out_ref, *, block):
    groups, tile_rows = out_ref.shape[0], out_ref.shape[1]
    per_row = LANES // block
    group_rows = groups // per_row
    stride = per_row * group_rows
    lane_part = iota((tile_rows, LANES), 1) // block
    for a in range(group_rows):
        x = [in_ref[pl.ds(q * group_rows + a, tile_rows, stride=stride), :] for q in range(per_row)]
        for b in range(per_row):
            y = None
            for q in range(per_row):
                shift = (block * (q - b)) % LANES
                moved = pltpu.roll(x[q], shift, axis=1) if shift else x[q]
                y = moved if y is None else jnp.where(lane_part == q, moved, y)
            out_ref[a * per_row + b, :, :] = y


def backdrop_kernel(signal_ref, peak_ref, extra_ref, iso_ref, kernel_ref, iso_kernel_ref, out_ref):
    num_bins = kernel_ref.shape[1]
    num_voxels = peak_ref.shape[1]
    bins = iota((num_bins, num_voxels), 0)
    extra_map = jnp.zeros((num_bins, num_voxels), F32)
    for k in range(peak_ref.shape[0]):
        extra_map += jnp.where(bins == peak_ref[k:k + 1, :], extra_ref[k:k + 1, :], 0.0)
    zeppelin = jnp.dot(kernel_ref[...], extra_map, precision=HIGH, preferred_element_type=F32)
    out_ref[...] = zeppelin + iso_kernel_ref[...] * iso_ref[...] - signal_ref[...].astype(F32)


def tile_kernel(arrived_ref, backdrop_ref, kernel_ref, residual_ref, back_ref, bins_ref,
                *, num_voxels, chunk):
    tiles = arrived_ref.shape[0]
    half = arrived_ref.shape[1] // 2
    num_bins = kernel_ref.shape[1]
    width = half * LANES
    bin_ids = iota((num_bins, LANES), 0)
    voxel_ids = iota((num_voxels, LANES), 0)

    def scatter(c, acc):
        picked = []
        for i in range(chunk):
            t = c * chunk + i
            for r in range(half):
                value = arrived_ref[t, r:r + 1, :]
                key = arrived_ref[t, half + r:half + r + 1, :].astype(jnp.int32)
                hot = (bin_ids == key // num_voxels).astype(F32).astype(BF16)
                bins_ref[c, :, (i * half + r) * LANES:(i * half + r + 1) * LANES] = hot
                spread = jnp.where(voxel_ids == key % num_voxels, value, 0.0)
                picked.append(jnp.concatenate(split2(spread), axis=0))
        return acc + dot(bins_ref[c], jnp.concatenate(picked, axis=1), ((1,), (1,)))

    acc = lax.fori_loop(0, tiles // chunk, scatter, jnp.zeros((num_bins, 2 * num_voxels), F32))
    fiber = acc[:, :num_voxels] + acc[:, num_voxels:]
    residual = jnp.dot(kernel_ref[...], fiber, precision=HIGH, preferred_element_type=F32)
    residual += backdrop_ref[...]
    residual_ref[...] = residual
    back = lax.dot_general(residual, kernel_ref[...], (((0,), (0,)), ((), ())),
                           precision=HIGH, preferred_element_type=F32)
    back = jnp.concatenate(split2(back), axis=0)

    def gather(c, carry):
        rows = dot(back, bins_ref[c], ((1,), (0,)))
        rows = rows[:num_voxels] + rows[num_voxels:]
        for i in range(chunk):
            t = c * chunk + i
            for r in range(half):
                key = arrived_ref[t, half + r:half + r + 1, :].astype(jnp.int32)
                at = (i * half + r) * LANES
                hit = jnp.where(voxel_ids == key % num_voxels, rows[:, at:at + LANES], 0.0)
                back_ref[t, r:r + 1, :] = jnp.sum(hit, axis=0, keepdims=True)
        return carry

    lax.fori_loop(0, tiles // chunk, gather, 0)


def extra_kernel_body(residual_ref, peak_ref, extra_ref, iso_ref, kernel_ref, iso_kernel_ref, step_ref,
                      new_extra_ref, new_iso_ref):
    num_bins = kernel_ref.shape[1]
    num_voxels = peak_ref.shape[1]
    step = step_ref[0]
    residual = residual_ref[...]
    back = lax.dot_general(kernel_ref[...], residual, (((0,), (0,)), ((), ())),
                           precision=HIGH, preferred_element_type=F32)
    bins = iota((num_bins, num_voxels), 0)
    for k in range(peak_ref.shape[0]):
        grad = jnp.sum(jnp.where(bins == peak_ref[k:k + 1, :], back, 0.0), axis=0, keepdims=True)
        new_extra_ref[k:k + 1, :] = jnp.maximum(extra_ref[k:k + 1, :] - step * grad, 0.0)
    grad = jnp.sum(iso_kernel_ref[...] * residual, axis=0, keepdims=True)
    new_iso_ref[...] = jnp.maximum(iso_ref[...] - step * grad, 0.0)


def stream_kernel(back_ref, length_ref, stream_ref, weight_ref, step_ref, out_ref, *, chunk):
    rows = length_ref.shape[0]
    side = 32
    ids = iota((side, LANES), 0)
    back = back_ref[...].reshape(rows, LANES)
    acc = jnp.zeros((side, 2 * side), F32)
    contrib = back * length_ref[...]
    stream = stream_ref[...]
    for c in range(rows // chunk):
        high, low = [], []
        for r in range(c * chunk, (c + 1) * chunk):
            s = stream[r:r + 1, :]
            high.append((ids == s // side).astype(F32).astype(BF16))
            spread = jnp.where(ids == s % side, contrib[r:r + 1, :], 0.0)
            low.append(jnp.concatenate(split2(spread), axis=0))
        acc += dot(jnp.concatenate(high, axis=1), jnp.concatenate(low, axis=1), ((1,), (1,)))
    grad = acc[:, :side] + acc[:, side:]
    per_row = LANES // side
    out_rows = out_ref.shape[0]
    lines = [jnp.concatenate([grad[per_row * r + q:per_row * r + q + 1, :] for q in range(per_row)], axis=1)
             for r in range(out_rows)]
    grad = jnp.concatenate(lines, axis=0)
    out_ref[...] = jnp.maximum(weight_ref[...] - step_ref[0] * grad, 0.0)


VMEM = pl.BlockSpec(memory_space=pltpu.VMEM)
SMEM = pl.BlockSpec(memory_space=pltpu.SMEM)


def call(kernel, out_shape, in_specs, name, scratch=(), limit=48):
    multi = isinstance(out_shape, (list, tuple))
    return pl.pallas_call(
        kernel,
        out_shape=out_shape,
        in_specs=in_specs,
        out_specs=[VMEM] * len(out_shape) if multi else VMEM,
        scratch_shapes=scratch,
        compiler_params=pltpu.CompilerParams(vmem_limit_bytes=limit * 1024 * 1024),
        name=name,
    )


def shape(dims, dtype=F32):
    return jax.ShapeDtypeStruct(dims, dtype)


def on_device(seg_stream, seg_voxel, seg_bin, seg_length, seg_count, stream_weight, signal, peak_bin,
              extra_weight, iso_weight, intra_kernel, extra_kernel, iso_kernel, step_size):
    groups = lax.axis_size("grp")
    tiles = lax.axis_size("tile")
    owners, block = seg_stream.shape[1:]
    num_dirs, num_bins = intra_kernel.shape
    num_voxels = signal.shape[1]
    num_streams = stream_weight.shape[0]
    rows = owners * block // LANES
    tile_rows = rows // groups
    group_rows = rows // tiles
    weight_rows = stream_weight.reshape(num_streams // LANES, LANES)
    iso_row = iso_weight.reshape(1, num_voxels)
    iso_column = iso_kernel.reshape(num_dirs, 1)

    outgoing, stream, length = call(
        lambda *refs: prepare_kernel(*refs, num_voxels=num_voxels),
        [shape((groups, 2 * tile_rows, LANES)), shape((rows, LANES), jnp.int32), shape((rows, LANES))],
        [VMEM] * 6, "prepare",
    )(seg_stream, seg_voxel, seg_bin, seg_length, seg_count, weight_rows)
    passing = lax.all_to_all(outgoing, "grp", split_axis=0, concat_axis=0, tiled=True)
    backdrop = call(backdrop_kernel, shape((num_dirs, num_voxels)), [VMEM] * 6, "backdrop")(
        signal, peak_bin, extra_weight, iso_row, extra_kernel, iso_column)
    regrouped = call(
        lambda *refs: regroup_kernel(*refs, block=block, arrays=2),
        shape((tiles * 2 * group_rows, LANES)), [VMEM], "regroup",
    )(passing)
    arrived = lax.all_to_all(regrouped.reshape(tiles, 2 * group_rows, LANES), "tile",
                             split_axis=0, concat_axis=0, tiled=True)
    chunk = 4
    residual, seg_back = call(
        lambda *refs: tile_kernel(*refs, num_voxels=num_voxels, chunk=chunk),
        [shape((num_dirs, num_voxels)), shape((tiles, group_rows, LANES))],
        [VMEM] * 3, "tile",
        scratch=[pltpu.VMEM((tiles // chunk, num_bins, chunk * group_rows * LANES), BF16)],
    )(arrived, backdrop, intra_kernel)
    returning = lax.all_to_all(seg_back, "tile", split_axis=0, concat_axis=0, tiled=True)
    new_extra, new_iso = call(
        extra_kernel_body, [shape(extra_weight.shape), shape((1, num_voxels))],
        [VMEM] * 6 + [SMEM], "extra",
    )(residual, peak_bin, extra_weight, iso_row, extra_kernel, iso_column, step_size)
    ungrouped = call(
        lambda *refs: ungroup_kernel(*refs, block=block),
        shape((groups, tile_rows, LANES)), [VMEM], "ungroup",
    )(returning.reshape(tiles * group_rows, LANES))
    returned = lax.all_to_all(ungrouped, "grp", split_axis=0, concat_axis=0, tiled=True)
    new_stream = call(
        lambda *refs: stream_kernel(*refs, chunk=16),
        shape(weight_rows.shape), [VMEM] * 4 + [SMEM], "streams",
    )(returned, length, stream, weight_rows, step_size)
    return (residual, new_stream.reshape(num_streams), new_extra, new_iso.reshape(num_voxels))


def solution(mesh):
    split = ("grp", "tile")
    return jax.shard_map(
        on_device,
        mesh=mesh,
        in_specs=(
            P(split, None, None),
            P(split, None, None),
            P(split, None, None),
            P(split, None, None),
            P(split, None),
            P(split),
            P(None, split),
            P(None, split),
            P(None, split),
            P(split),
            P(),
            P(),
            P(),
            P(),
        ),
        out_specs=(
            P(None, split),
            P(split),
            P(None, split),
            P(split),
        ),
        check_vma=False,
    )
```

time: 467 us -> 98.7 us (0.21)
  other arithmetic: 208 us -> 0 us
  local copies, waits for them, and re-layouts: 171 us -> 3.47 us
  blocking collectives: 0 us -> 38.6 us
  starting transfers between devices: 50.1 us -> 14.4 us
  Pallas kernels: 0 us -> 24 us
  waiting for transfers between devices: 32.3 us -> 16.2 us
    scatter-add x2 -> x0, other arithmetic: 199 us -> none  [the longest x1 113 us: on_device(): jax.ops.segment_sum(contrib.reshape(-1), seg_stream[0].reshape(-1), num_s...]
    gather x5 -> x0, local copies, waits for them, and re-layouts: 159 us -> none  [the longest x2 90.7 us: on_device(): jnp.take(intra_back.reshape(-1), flat_keys).reshape(arrived_keys.shape)]
    all_to_all x0 -> x2, blocking collectives: none -> 38.6 us  [the longest x1 27.7 us: on_device(): lax.all_to_all(outgoing, 'grp', split_axis=0, concat_axis=0, tiled=True)]
    all_to_all x6 -> x2, starting transfers between devices: 50.1 us -> 14.4 us  [the longest x1 10.9 us: on_device(): lax.all_to_all(regrouped.reshape(tiles, 2 * group_rows, LANES), 'tile', s...]
    pallas_call x0 -> x7, Pallas kernels: none -> 24 us  [the longest x1 18 us: on_device(): call(lambda *refs: tile_kernel(*refs, num_voxels=num_voxels, chunk=chunk)...]
    all_to_all x6 -> x2, waiting for transfers between devices: 32.3 us -> 16.2 us  [the longest x1 9.45 us: on_device(): lax.all_to_all(ungrouped, 'grp', split_axis=0, concat_axis=0, tiled=True)]
    all_to_all x6 -> x0, other arithmetic: 4.83 us -> none  [the longest x1 0.81 us: send_forward(): lax.all_to_all(lax.all_to_all(outgoing[1], 'grp', split_axis=0, concat_ax...]
    unnamed x40 -> x30, local copies, waits for them, and re-layouts: 8.14 us -> 3.38 us
  transfers between devices with their start and end apart: 6 -> 2, of which waited for: 5 -> 2; matrix products, arithmetic and copies ran while one was open for 17% -> 0% of each run, Pallas kernels for 0% -> 2%
where the time goes in v1:
time: 98.7 us; the launch traced here: 98.2 us
  blocking collectives  38.6 us (39%)
  Pallas kernels  24 us (24%)
  waiting for transfers between devices  16.2 us (16%)
  starting transfers between devices  14.4 us (15%)
  local copies, waits for them, and re-layouts  3.47 us (4%)
  between operations  1.47 us (1%)
    all_to_all x1, blocking collectives, on_device(): lax.all_to_all(outgoing, 'grp', split_axis=0, concat_axis=0, tiled=True)  27.7 us
    pallas_call x1, Pallas kernels, on_device(): call(lambda *refs: tile_kernel(*refs, num_voxels=num_voxels, chunk=chunk)...  18 us
    all_to_all x1, blocking collectives, on_device(): lax.all_to_all(seg_back, 'tile', split_axis=0, concat_axis=0, tiled=True)  10.9 us
    all_to_all x1, starting transfers between devices, on_device(): lax.all_to_all(regrouped.reshape(tiles, 2 * group_rows, LANES), 'tile', s...  10.9 us
    all_to_all x1, waiting for transfers between devices, on_device(): lax.all_to_all(ungrouped, 'grp', split_axis=0, concat_axis=0, tiled=True)  9.45 us
    all_to_all x1, waiting for transfers between devices, on_device(): lax.all_to_all(regrouped.reshape(tiles, 2 * group_rows, LANES), 'tile', s...  6.8 us
    all_to_all x1, starting transfers between devices, on_device(): lax.all_to_all(ungrouped, 'grp', split_axis=0, concat_axis=0, tiled=True)  3.55 us
    unnamed x30, local copies, waits for them, and re-layouts  3.38 us
  transfers between devices with their start and end apart: 2, of which 2 were waited for; matrix products, arithmetic and copies ran while one was open for 0% of the time, Pallas kernels for 2%

profile of v1, /device:TPU:1, one launch (start us, length us, event | category | flops | bytes accessed | tf_op | source)
XLA Modules:
  0.0 98.2 jit_solution(1042252799641013420)
XLA Ops:
  0.6 1.0 %copy.22.refs_0_ = s32[1,512,32]{2,1,0:T(8,128)S(1)} copy(s32[1,512,32]{1,2,0:T(8,128)} %param.14) | data formatting | bytes 131072 | tf_op args[0]
  1.7 0.1 copy.23.refs_1_
  1.8 0.7 copy-done.10
  2.5 0.1 copy.24.refs_2_
  2.6 0.7 copy-done.11
  3.3 0.1 copy.25.refs_3_
  3.5 0.6 copy-done.4
  4.0 0.0 copy-done.8
  4.0 0.7 prepare.1
  4.7 0.0 copy-start
  4.7 27.7 %all_to_all.20.refs_0_ = f32[16,16,128]{2,1,0:T(8,128)S(1)} all-to-all(f32[16,16,128]{2,1,0:T(8,128)S(1)} %get-tuple-element.11), channel_id=1, replica_groups=mesh['grp'=16,'tile'=32] {'grp'}, dimensions={0} | all-to-all | bytes 262144 | tf_op jit(solution)/shard_map/all_to_all | solution.py:239
  32.4 0.8 regroup.1
  33.2 0.0 copy-start.7
  33.2 10.9 %all-to-all-start.1 = ((f32[32,8,128]{2,1,0:T(8,128)}), f32[32,8,128]{2,1,0:T(8,128)S(1)}, u32[]{:S(2)}, u32[]{:S(2)}) async-start(f32[32,8,128]{2,1,0:T(8,128)} %bitcast.1), calls=%async_computation.1 | async-start | bytes 262144 | tf_op jit(solution)/shard_map/all_to_all | solution.py:246
  44.1 0.1 reshape.36.iso_kernel_ref
  44.3 0.7 backdrop.1.refs_1_
  45.0 6.8 %all-to-all-done.1.refs_0_ = f32[32,8,128]{2,1,0:T(8,128)S(1)} async-done(((f32[32,8,128]{2,1,0:T(8,128)}), f32[32,8,128]{2,1,0:T(8,128)S(1)}, u32[]{:S(2)}, u32[]{:S(2)}) %all-to-all-start.1) | async-done | bytes 131104 | tf_op jit(solution)/shard_map/all_to_all | solution.py:246
  51.8 18.0 %tile.1 = (f32[288,128]{1,0:T(8,128)}, f32[32,4,128]{2,1,0:T(4,128)S(1)}) custom-call(f32[32,8,128]{2,1,0:T(8,128)S(1)} %all-to-all-done.1.refs_0_, f32[288,128]{1,0:T(8,128)S(1)} %backdrop.1.refs_1_, f32[288,512]{1,0:T(8,128)S(1)} %copy-done.1), custom_call_target="tpu_custom_call" | custom-call | tf_op jit(solution)/shard_map/tile/pallas_call | solution.py:249
  69.8 10.9 %all_to_all.21 = f32[32,4,128]{2,1,0:T(4,128)S(1)} all-to-all(f32[32,4,128]{2,1,0:T(4,128)S(1)} %get-tuple-element.13), channel_id=1, replica_groups=mesh['grp'=16,'tile'=32] {'tile'}, dimensions={0} | all-to-all | bytes 131072 | tf_op jit(solution)/shard_map/all_to_all | solution.py:255
  80.8 0.7 ungroup.1
  81.5 3.6 %all-to-all-start.3 = ((f32[16,8,128]{2,1,0:T(8,128)}), f32[16,8,128]{2,1,0:T(8,128)S(1)}, u32[]{:S(2)}, u32[]{:S(2)}) async-start(f32[16,8,128]{2,1,0:T(8,128)} %ungroup.1), calls=%async_computation.3 | async-start | bytes 131072 | tf_op jit(solution)/shard_map/all_to_all | solution.py:264
  85.8 1.5 %extra.1 = (f32[3,128]{1,0:T(4,128)}, f32[1,128]{1,0:T(1,128)}) custom-call(f32[288,128]{1,0:T(8,128)S(1)} %copy-done.2, s32[3,128]{1,0:T(4,128)S(1)} %copy-done.5, f32[3,128]{1,0:T(4,128)S(1)} %copy-done.6, f32[1,128]{1,0:T(1,128)S(1)} %bitcast.10, f32[288,512]{1,0:T(8,128)S(1)} %copy-done, f32[288,1]{1,0:T(8,128)S(1)} %reshape.36.iso_kernel_ref, ...), custom_call_target="tpu_custom_call" | custom-call | tf_op jit(solution)/shard_map/extra/pallas_call | solution.py:256
  87.2 9.4 %all-to-all-done.3.refs_0_ = f32[16,8,128]{2,1,0:T(8,128)S(1)} async-done(((f32[16,8,128]{2,1,0:T(8,128)}), f32[16,8,128]{2,1,0:T(8,128)S(1)}, u32[]{:S(2)}, u32[]{:S(2)}) %all-to-all-start.3) | async-done | bytes 65568 | tf_op jit(solution)/shard_map/all_to_all | solution.py:264
  96.7 1.5 %streams.1 = f32[8,128]{1,0:T(8,128)} custom-call(f32[16,8,128]{2,1,0:T(8,128)S(1)} %all-to-all-done.3.refs_0_, f32[128,128]{1,0:T(8,128)S(1)} %get-tuple-element.14.refs_1_, s32[128,128]{1,0:T(8,128)S(1)} %get-tuple-element.15.refs_2_, f32[8,128]{1,0:T(8,128)S(1)} %bitcast.8, f32[1]{0:T(128)S(6)} %copy.28.refs_4_.step_ref), custom_call_target="tpu_custom_call" | custom-call | tf_op jit(solution)/shard_map/streams/pallas_call | solution.py:265
  (20 shorter events, 0.0 us)
Async XLA Ops:
  0.6 1.0 %copy-start.9 = (s32[1,512,32]{1,2,0:T(8,128)S(1)}, s32[1,512,32]{1,2,0:T(8,128)}, u32[]{:S(2)}) copy-start(s32[1,512,32]{1,2,0:T(8,128)} %param.15) | copy-start | bytes 196612
  1.6 0.8 copy-start.10
  2.5 0.8 copy-start.11
  3.3 0.7 copy-start.4
  3.3 0.7 copy-start.8
  4.7 39.6 %copy-start = (f32[288,512]{1,0:T(8,128)S(1)}, f32[288,512]{1,0:T(8,128)}, u32[]{:S(2)}) copy-start(f32[288,512]{1,0:T(8,128)} %kernel_ref.3) | copy-start | bytes 1769476
  33.2 10.9 %copy-start.12 = (f32[288]{0:T(512)S(1)}, f32[288]{0:T(512)}, u32[]{:S(2)}) copy-start(f32[288]{0:T(512)} %param.26) | copy-start | bytes 3460
  33.2 11.0 %copy-start.3 = (bf16[288,128]{1,0:T(8,128)(2,1)S(1)}, bf16[288,128]{1,0:T(8,128)(2,1)}, u32[]{:S(2)}) copy-start(bf16[288,128]{1,0:T(8,128)(2,1)} %signal_ref.1) | copy-start | bytes 221188
  33.2 11.1 %copy-start.5 = (s32[3,128]{1,0:T(4,128)S(1)}, s32[3,128]{1,0:T(4,128)}, u32[]{:S(2)}) copy-start(s32[3,128]{1,0:T(4,128)} %peak_ref.3) | copy-start | bytes 4612
  33.2 11.1 %copy-start.6 = (f32[3,128]{1,0:T(4,128)S(1)}, f32[3,128]{1,0:T(4,128)}, u32[]{:S(2)}) copy-start(f32[3,128]{1,0:T(4,128)} %extra_ref.3) | copy-start | bytes 4612
  33.2 11.1 %copy-start.7 = (f32[128]{0:T(128)S(1)}, f32[128]{0:T(128)}, u32[]{:S(2)}) copy-start(f32[128]{0:T(128)} %param.23) | copy-start | bytes 1540
  33.2 18.6 %all-to-all-start.1 = ((f32[32,8,128]{2,1,0:T(8,128)}), f32[32,8,128]{2,1,0:T(8,128)S(1)}, u32[]{:S(2)}, u32[]{:S(2)}) async-start(f32[32,8,128]{2,1,0:T(8,128)} %bitcast.1), calls=%async_computation.1 | async-start | bytes 262144 | tf_op jit(solution)/shard_map/all_to_all | solution.py:246
  44.1 7.7 %copy-start.1 = (f32[288,512]{1,0:T(8,128)S(1)}, f32[288,512]{1,0:T(8,128)}, u32[]{:S(2)}) copy-start(f32[288,512]{1,0:T(8,128)} %refs_2_.2) | copy-start | bytes 1769476
  80.8 5.0 %copy-start.2 = (f32[288,128]{1,0:T(8,128)S(1)}, f32[288,128]{1,0:T(8,128)}, u32[]{:S(2)}) copy-start(f32[288,128]{1,0:T(8,128)} %get-tuple-element.7.residual_ref) | copy-start | bytes 442372
  81.5 15.2 %all-to-all-start.3 = ((f32[16,8,128]{2,1,0:T(8,128)}), f32[16,8,128]{2,1,0:T(8,128)S(1)}, u32[]{:S(2)}, u32[]{:S(2)}) async-start(f32[16,8,128]{2,1,0:T(8,128)} %ungroup.1), calls=%async_computation.3 | async-start | bytes 131072 | tf_op jit(solution)/shard_map/all_to_all | solution.py:264

commit v2 on v1

v2 whole, which is shorter than its diff:
```python
import jax
import jax.numpy as jnp
from jax import lax
from jax.experimental import pallas as pl
from jax.experimental.pallas import tpu as pltpu
from jax.sharding import Mesh, PartitionSpec as P

LANES = 128
CORES = 2
CHUNK = 64
F32 = jnp.float32
BF16 = jnp.bfloat16
I16 = jnp.int16
HIGH = lax.Precision.HIGHEST


def iota(shape, dim):
    return lax.broadcasted_iota(jnp.int32, shape, dim)


def split2(x):
    head = x.astype(BF16)
    return head, (x - head.astype(F32)).astype(BF16)


def dot(a, b, dims):
    return lax.dot_general(a, b, (dims, ((), ())), preferred_element_type=F32)


def roll(x, shift):
    shift = shift % LANES
    return pltpu.roll(x, shift, axis=1) if shift else x


def side_by_side(parts, width, offset=0):
    lane_part = iota(parts[0].shape, 1) // width
    out = None
    for i, part in enumerate(parts):
        moved = roll(part, width * i - offset)
        out = moved if out is None else jnp.where(lane_part == i, moved, out)
    return out


def live_length(length_ref, count_ref):
    length = length_ref[0]
    return jnp.where(iota(length.shape, 0) < count_ref[...], length, 0.0)


def turned(a, b):
    pad = jnp.zeros((LANES - 2 * a.shape[0], LANES), F32)
    return jnp.transpose(jnp.concatenate([a, b, pad], axis=0))


def prepare_kernel(stream_hbm, voxel_hbm, bin_hbm, length_hbm, count_hbm, weight_hbm,
                   out_ref, turned_ref, stream_ref, voxel_ref, bin_ref, length_ref, count_ref, weight_ref,
                   sems, *, num_voxels):
    copies = [
        pltpu.make_async_copy(source, target, sems.at[i])
        for i, (source, target) in enumerate((
            (stream_hbm, stream_ref), (weight_hbm, weight_ref), (count_hbm, count_ref),
            (length_hbm, length_ref), (bin_hbm, bin_ref), (voxel_hbm, voxel_ref)))
    ]
    for copy in copies:
        copy.start()
    for copy in copies:
        copy.wait()
    block, owners = stream_ref.shape[1:]
    length = live_length(length_ref, count_ref)
    keys = (bin_ref[0] * num_voxels + voxel_ref[0]).astype(F32)
    tables = [jnp.broadcast_to(weight_ref[r:r + 1, :], (block, LANES)) for r in range(weight_ref.shape[0])]
    for start in range(0, owners, LANES):
        stream = stream_ref[0, :, start:start + LANES]
        lane_id = stream % LANES
        row_id = stream // LANES
        weight = jnp.zeros((block, LANES), F32)
        for r, table in enumerate(tables):
            weight = jnp.where(row_id == r, jnp.take_along_axis(table, lane_id, axis=1), weight)
        turned_ref[start:start + LANES, :] = turned(
            weight * length[:, start:start + LANES], keys[:, start:start + LANES])
    chips = owners // CORES
    out_ref[...] = side_by_side(
        [turned_ref[pl.ds(core, chips, stride=CORES), :] for core in range(CORES)], 2 * block)


def slots_kernel(stream_ref, length_ref, count_ref, stream_out_ref, length_out_ref, *, tiles):
    block, owners = stream_ref.shape[1:]
    length = live_length(length_ref, count_ref)
    stream = stream_ref[0].astype(F32)
    per_row = LANES // block
    height = tiles // per_row
    for start in range(0, owners, LANES):
        both = turned(stream[:, start:start + LANES], length[:, start:start + LANES])
        for first in range(0, LANES, tiles):
            parts = [both[first + u * height:first + (u + 1) * height, :] for u in range(per_row)]
            row = (start + first) // tiles * height
            stream_out_ref[row:row + height, :] = side_by_side(parts, block).astype(jnp.int32)
            length_out_ref[row:row + height, :] = side_by_side(parts, block, block)


def backdrop_kernel(signal_ref, peak_ref, extra_ref, iso_ref, kernel_ref, iso_kernel_ref, intra_ref,
                    out_ref, parts_ref):
    num_bins = kernel_ref.shape[1]
    num_voxels = peak_ref.shape[1]
    bins = iota((num_bins, num_voxels), 0)
    extra_map = jnp.zeros((num_bins, num_voxels), F32)
    for k in range(peak_ref.shape[0]):
        extra_map += jnp.where(bins == peak_ref[k:k + 1, :], extra_ref[k:k + 1, :], 0.0)
    zeppelin = jnp.dot(kernel_ref[...], extra_map, precision=HIGH, preferred_element_type=F32)
    out_ref[...] = zeppelin + iso_kernel_ref[...] * iso_ref[...] - signal_ref[...].astype(F32)
    parts_ref[0], parts_ref[1] = split2(intra_ref[...])


def tile_kernel(own_ref, other_ref, backdrop_ref, parts_ref, core_ref, residual_ref, back_ref,
                value_ref, key_ref, found_ref, *, num_voxels, block, group_rows):
    chips = own_ref.shape[0]
    num_bins = parts_ref.shape[2]
    per_row = LANES // block
    rows = chips // per_row
    places = rows // group_rows
    chunks, chunk = key_ref.shape[:2]
    bin_ids = iota((num_bins, LANES), 0).astype(I16)
    voxel_ids = iota((num_voxels, LANES), 0).astype(I16)
    voxel_ids32 = iota((num_voxels, LANES), 0)
    one, zero = jnp.ones((), BF16), jnp.zeros((), BF16)

    for source, ref in enumerate((own_ref, other_ref)):
        mine = ref[...]
        mine = jnp.where(core_ref[0] == 0, mine, pltpu.roll(mine, LANES // CORES, axis=1))
        quarters = [mine[b * rows:(b + 1) * rows, :] for b in range(per_row)]
        value = side_by_side(quarters, block)
        key = side_by_side(quarters, block, block)
        for start in range(0, rows, chunk):
            value_ref[(source * rows + start) // chunk] = value[start:start + chunk]
            key_ref[(source * rows + start) // chunk] = key[start:start + chunk].astype(jnp.int32)

    def hots(c):
        return jnp.concatenate([
            jnp.where(bin_ids == (key_ref[c, i:i + 1, :] // num_voxels).astype(I16), one, zero)
            for i in range(chunk)], axis=1)

    def scatter(c, acc):
        spread = []
        for i in range(chunk):
            head, tail = split2(value_ref[c, i:i + 1, :])
            here = voxel_ids == (key_ref[c, i:i + 1, :] % num_voxels).astype(I16)
            spread.append(jnp.concatenate([jnp.where(here, head, zero), jnp.where(here, tail, zero)], axis=0))
        return acc + dot(hots(c), jnp.concatenate(spread, axis=1), ((1,), (1,)))

    acc = lax.fori_loop(0, chunks, scatter, jnp.zeros((num_bins, 2 * num_voxels), F32))
    fiber = jnp.concatenate(split2(acc[:, :num_voxels] + acc[:, num_voxels:]), axis=1)
    product = dot(parts_ref[0], fiber, ((1,), (0,))) + dot(parts_ref[1], fiber, ((1,), (0,)))
    residual = product[:, :num_voxels] + product[:, num_voxels:] + backdrop_ref[...]
    residual_ref[...] = residual
    turned_residual = jnp.concatenate(split2(jnp.transpose(residual)), axis=0)
    product = dot(turned_residual, parts_ref[0], ((1,), (0,))) + dot(turned_residual, parts_ref[1], ((1,), (0,)))
    back = jnp.concatenate(split2(product[:num_voxels] + product[num_voxels:]), axis=0)

    def gather(c, carry):
        found = dot(back, hots(c), ((1,), (0,)))
        found = found[:num_voxels] + found[num_voxels:]
        for i in range(chunk):
            hit = jnp.where(voxel_ids32 == key_ref[c, i:i + 1, :] % num_voxels,
                            found[:, i * LANES:(i + 1) * LANES], 0.0)
            found_ref[c, i:i + 1, :] = jnp.sum(hit, axis=0, keepdims=True)
        return carry

    lax.fori_loop(0, chunks, gather, 0)
    for source in range(CORES):
        source_core = core_ref[0] if source == 0 else 1 - core_ref[0]
        for a in range(group_rows):
            n = source * rows + a * places
            back_ref[pl.ds(source_core * group_rows + a, places, stride=CORES * group_rows), :] = (
                found_ref[n // chunk, n % chunk:n % chunk + places, :])


def ungroup_kernel(in_ref, out_ref, *, block):
    groups, height = out_ref.shape[0], out_ref.shape[1]
    per_row = LANES // block
    group_rows = groups // per_row
    for a in range(group_rows):
        parts = [in_ref[pl.ds(u * height * group_rows + a, height, stride=group_rows), :]
                 for u in range(per_row)]
        for b in range(per_row):
            out_ref[b * group_rows + a] = side_by_side([roll(part, -block * b) for part in parts], block)


def extra_kernel_body(residual_ref, peak_ref, extra_ref, iso_ref, kernel_ref, iso_kernel_ref, step_ref,
                      new_extra_ref, new_iso_ref):
    num_bins = kernel_ref.shape[1]
    num_voxels = peak_ref.shape[1]
    step = step_ref[0]
    residual = residual_ref[...]
    back = lax.dot_general(kernel_ref[...], residual, (((0,), (0,)), ((), ())),
                           precision=HIGH, preferred_element_type=F32)
    bins = iota((num_bins, num_voxels), 0)
    for k in range(peak_ref.shape[0]):
        grad = jnp.sum(jnp.where(bins == peak_ref[k:k + 1, :], back, 0.0), axis=0, keepdims=True)
        new_extra_ref[k:k + 1, :] = jnp.maximum(extra_ref[k:k + 1, :] - step * grad, 0.0)
    grad = jnp.sum(iso_kernel_ref[...] * residual, axis=0, keepdims=True)
    new_iso_ref[...] = jnp.maximum(iso_ref[...] - step * grad, 0.0)


def stream_kernel(back_ref, length_ref, stream_ref, weight_ref, step_ref, out_ref):
    rows = length_ref.shape[0]
    side = 32
    ids = iota((side, LANES), 0).astype(I16)
    one, zero = jnp.ones((), BF16), jnp.zeros((), BF16)
    contrib = back_ref[...].reshape(rows, LANES) * length_ref[...]
    stream = stream_ref[...]
    major, minor = stream // side, stream % side
    high, low = [], []
    for r in range(rows):
        high.append(jnp.where(ids == major[r:r + 1, :].astype(I16), one, zero))
        here = ids == minor[r:r + 1, :].astype(I16)
        head, tail = split2(contrib[r:r + 1, :])
        low.append(jnp.concatenate([jnp.where(here, head, zero), jnp.where(here, tail, zero)], axis=0))
    acc = dot(jnp.concatenate(high, axis=1), jnp.concatenate(low, axis=1), ((1,), (1,)))
    grad = acc[:, :side] + acc[:, side:]
    per_row = LANES // side
    lines = [jnp.concatenate([grad[per_row * r + q:per_row * r + q + 1, :] for q in range(per_row)], axis=1)
             for r in range(out_ref.shape[0])]
    grad = jnp.concatenate(lines, axis=0)
    out_ref[...] = jnp.maximum(weight_ref[...] - step_ref[0] * grad, 0.0)


VMEM = pl.BlockSpec(memory_space=pltpu.VMEM)
HBM = pl.BlockSpec(memory_space=pltpu.HBM)
SMEM = pl.BlockSpec(memory_space=pltpu.SMEM)


def call(kernel, out_shape, in_specs, name, scratch=(), limit=16):
    multi = isinstance(out_shape, (list, tuple))
    return pl.pallas_call(
        kernel,
        out_shape=out_shape,
        in_specs=in_specs,
        out_specs=[VMEM] * len(out_shape) if multi else VMEM,
        scratch_shapes=scratch,
        compiler_params=pltpu.CompilerParams(vmem_limit_bytes=limit * 1024 * 1024),
        name=name,
    )


def shape(dims, dtype=F32):
    return jax.ShapeDtypeStruct(dims, dtype)


def on_device(seg_stream, seg_voxel, seg_bin, seg_length, seg_count, stream_weight, signal, peak_bin,
              extra_weight, iso_weight, intra_kernel, extra_kernel, iso_kernel, step_size):
    groups = lax.axis_size("grp")
    tiles = lax.axis_size("place") * CORES
    owners, block = seg_stream.shape[1:]
    num_dirs, num_bins = intra_kernel.shape
    num_voxels = signal.shape[1]
    num_streams = stream_weight.shape[0]
    chips = owners // CORES
    rows = owners * block // LANES
    tile_rows = rows // groups
    group_rows = rows // tiles
    weight_rows = stream_weight.reshape(num_streams // LANES, LANES)
    iso_row = iso_weight.reshape(1, num_voxels)
    iso_column = iso_kernel.reshape(num_dirs, 1)
    core = lax.axis_index("core").astype(jnp.int32).reshape(1)
    by_slot = [jnp.swapaxes(x, 1, 2) for x in (seg_stream, seg_voxel, seg_bin, seg_length)]

    outgoing = call(
        lambda *refs: prepare_kernel(*refs, num_voxels=num_voxels),
        shape((chips, LANES)), [HBM] * 6, "prepare",
        scratch=[pltpu.VMEM((owners, LANES), F32)]
        + [pltpu.VMEM((1, block, owners), jnp.int32)] * 3
        + [pltpu.VMEM((1, block, owners), F32), pltpu.VMEM((1, owners), jnp.int32),
           pltpu.VMEM(weight_rows.shape, F32), pltpu.SemaphoreType.DMA((6,))],
    )(*(pltpu.with_memory_space_constraint(x, pltpu.HBM) for x in (*by_slot, seg_count, weight_rows)))
    own = lax.all_to_all(outgoing.reshape(chips, 1, LANES), ("grp", "place"),
                         split_axis=0, concat_axis=0, tiled=True).reshape(chips, LANES)
    stream, length = call(
        lambda *refs: slots_kernel(*refs, tiles=tiles),
        [shape((rows, LANES), jnp.int32), shape((rows, LANES))], [VMEM] * 3, "slots",
    )(by_slot[0], by_slot[3], seg_count)
    backdrop, parts = call(
        backdrop_kernel, [shape((num_dirs, num_voxels)), shape((2, num_dirs, num_bins), BF16)],
        [VMEM] * 7, "backdrop",
    )(signal, peak_bin, extra_weight, iso_row, extra_kernel, iso_column, intra_kernel)
    chunked = (rows // CHUNK, CHUNK, LANES)
    own, stream, length, backdrop, parts = lax.optimization_barrier((own, stream, length, backdrop, parts))
    other = lax.ppermute(own, "core", [(0, 1), (1, 0)])
    residual, seg_back = call(
        lambda *refs: tile_kernel(*refs, num_voxels=num_voxels, block=block, group_rows=group_rows),
        [shape((num_dirs, num_voxels)), shape((rows, LANES))], [VMEM] * 4 + [SMEM], "tile",
        scratch=[pltpu.VMEM(chunked, F32), pltpu.VMEM(chunked, jnp.int32), pltpu.VMEM(chunked, F32)],
        limit=32,
    )(own, other, backdrop, parts, core)
    returning = lax.all_to_all(seg_back.reshape(tiles, group_rows, LANES), ("place", "core"), split_axis=0, concat_axis=0, tiled=True)
    new_extra, new_iso = call(
        extra_kernel_body, [shape(extra_weight.shape), shape((1, num_voxels))],
        [VMEM] * 6 + [SMEM], "extra",
    )(residual, peak_bin, extra_weight, iso_row, extra_kernel, iso_column, step_size)
    ungrouped = call(
        lambda *refs: ungroup_kernel(*refs, block=block),
        shape((groups, tile_rows, LANES)), [VMEM], "ungroup",
    )(returning.reshape(tiles * group_rows, LANES))
    returned = lax.all_to_all(ungrouped, "grp", split_axis=0, concat_axis=0, tiled=True)
    new_stream = call(
        stream_kernel, shape(weight_rows.shape), [VMEM] * 4 + [SMEM], "streams",
    )(returned, length, stream, weight_rows, step_size)
    return (residual, new_stream.reshape(num_streams), new_extra, new_iso.reshape(num_voxels))


def solution(mesh):
    groups, tiles = mesh.devices.shape
    split = ("grp", "place", "core")
    return jax.shard_map(
        on_device,
        mesh=Mesh(mesh.devices.reshape(groups, tiles // CORES, CORES), split),
        in_specs=(
            P(split, None, None),
            P(split, None, None),
            P(split, None, None),
            P(split, None, None),
            P(split, None),
            P(split),
            P(None, split),
            P(None, split),
            P(None, split),
            P(split),
            P(),
            P(),
            P(),
            P(),
        ),
        out_specs=(
            P(None, split),
            P(split),
            P(None, split),
            P(split),
        ),
        check_vma=False,
    )
```

time: 98.7 us -> 89.7 us (0.909)
  blocking collectives: 38.6 us -> 10.9 us
  starting transfers between devices: 14.4 us -> 34.3 us
  Pallas kernels: 24 us -> 18.2 us
  waiting for transfers between devices: 16.2 us -> 21.1 us
    all_to_all x2 -> x1, blocking collectives: 38.6 us -> 10.9 us  [on_device(): lax.all_to_all(seg_back.reshape(tiles, group_rows, LANES), ('place', 'cor...]
    all_to_all x1, starting transfers between devices: 10.9 us -> 25.5 us  [on_device(): lax.all_to_all(outgoing.reshape(chips, 1, LANES), ('grp', 'place'), split...]
    pallas_call x5, Pallas kernels: 21.7 us -> 15.9 us  [the longest x1 11.1 us: on_device(): call(lambda *refs: tile_kernel(*refs, num_voxels=num_voxels, block=block,...]
    ppermute x0 -> x1, starting transfers between devices: none -> 5.34 us  [on_device(): other = lax.ppermute(own, 'core', [(0, 1), (1, 0)])]
    all_to_all x1, waiting for transfers between devices: 6.8 us -> 10.7 us  [on_device(): lax.all_to_all(outgoing.reshape(chips, 1, LANES), ('grp', 'place'), split...]
    unnamed x30 -> x24, local copies, waits for them, and re-layouts: 3.38 us -> 3.12 us
  transfers between devices with their start and end apart: 2 -> 3, of which waited for: 2 -> 3; matrix products, arithmetic and copies ran while one was open for 0% -> 0% of each run, Pallas kernels for 2% -> 3%
where the time goes in v2:
time: 89.7 us; the launch traced here: 89.2 us
  starting transfers between devices  34.3 us (38%)
  waiting for transfers between devices  21.1 us (24%)
  Pallas kernels  18.2 us (20%)
  blocking collectives  10.9 us (12%)
  local copies, waits for them, and re-layouts  3.21 us (4%)
  between operations  1.43 us (2%)
    all_to_all x1, starting transfers between devices, on_device(): lax.all_to_all(outgoing.reshape(chips, 1, LANES), ('grp', 'place'), split...  25.5 us
    pallas_call x1, Pallas kernels, on_device(): call(lambda *refs: tile_kernel(*refs, num_voxels=num_voxels, block=block,...  11.1 us
    all_to_all x1, blocking collectives, on_device(): lax.all_to_all(seg_back.reshape(tiles, group_rows, LANES), ('place', 'cor...  10.9 us
    all_to_all x1, waiting for transfers between devices, on_device(): lax.all_to_all(outgoing.reshape(chips, 1, LANES), ('grp', 'place'), split...  10.7 us
    all_to_all x1, waiting for transfers between devices, on_device(): lax.all_to_all(ungrouped, 'grp', split_axis=0, concat_axis=0, tiled=True)  9.48 us
    ppermute x1, starting transfers between devices, on_device(): other = lax.ppermute(own, 'core', [(0, 1), (1, 0)])  5.34 us
    all_to_all x1, starting transfers between devices, on_device(): lax.all_to_all(ungrouped, 'grp', split_axis=0, concat_axis=0, tiled=True)  3.49 us
    unnamed x24, local copies, waits for them, and re-layouts  3.12 us
  transfers between devices with their start and end apart: 3, of which 3 were waited for; matrix products, arithmetic and copies ran while one was open for 0% of the time, Pallas kernels for 3%

profile of v2, /device:TPU:1, one launch (start us, length us, event | category | flops | bytes accessed | tf_op | source)
XLA Modules:
  0.0 89.2 jit_solution(1284380738295234947)
XLA Ops:
  0.6 2.3 %prepare.1 = f32[256,128]{1,0:T(8,128)} custom-call(s32[1,32,512]{2,1,0:T(8,128)} %bitcast.17, s32[1,32,512]{2,1,0:T(8,128)} %bitcast.27, s32[1,32,512]{2,1,0:T(8,128)} %bitcast.28, f32[1,32,512]{2,1,0:T(8,128)} %bitcast.19, s32[1,512]{1,0:T(1,128)} %refs_2_.1, f32[8,128]{1,0:T(8,128)} %bitcast.23), custom_call_target="tpu_custom_call" | custom-call | tf_op jit(solution)/shard_map/prepare/pallas_call | solution.py:266
  3.0 0.0 copy-start.2
  3.0 0.0 copy-start.7
  3.0 25.5 %all-to-all-start = ((f32[256,1,128]{2,1,0:T(1,128)}), f32[256,1,128]{2,1,0:T(1,128)S(1)}, u32[]{:S(2)}, u32[]{:S(2)}) async-start(f32[256,1,128]{2,1,0:T(1,128)} %bitcast.6), calls=%async_computation | async-start | bytes 262144 | tf_op jit(solution)/shard_map/all_to_all | solution.py:274
  28.5 0.0 copy-start.3
  28.5 0.8 copy-done.3
  29.3 0.3 slots.1
  29.6 0.4 copy-done.11
  30.0 0.1 reshape.48.iso_kernel_ref
  30.1 0.0 copy-start.10
  30.1 0.8 copy-done.5
  30.9 1.1 %copy-done.1 = f32[288,512]{1,0:T(8,128)S(1)} copy-done((f32[288,512]{1,0:T(8,128)S(1)}, f32[288,512]{1,0:T(8,128)}, u32[]{:S(2)}) %copy-start.1) | copy-done | bytes 589848
  32.0 0.8 backdrop.1
  32.8 10.7 %all-to-all-done = f32[256,1,128]{2,1,0:T(1,128)S(1)} async-done(((f32[256,1,128]{2,1,0:T(1,128)}), f32[256,1,128]{2,1,0:T(1,128)S(1)}, u32[]{:S(2)}, u32[]{:S(2)}) %all-to-all-start) | async-done | bytes 131104 | tf_op jit(solution)/shard_map/all_to_all | solution.py:274
  43.5 5.3 %collective-permute-start = (f32[256,128]{1,0:T(8,128)S(1)}, f32[256,128]{1,0:T(8,128)S(1)}, u32[]{:S(2)}, u32[]{:S(2)}) collective-permute-start(f32[256,128]{1,0:T(8,128)S(1)} %bitcast.15), channel_id=1, source_target_pairs={{0,1},{1,0},{2,3},{3,2},{4,5},{5,4},{6,7},{7,6},{8,9},{9,8},{10,11... | collective-permute-start | bytes 393224 | tf_op jit(solution)/shard_map/ppermute | solution.py:286
  48.8 1.0 %collective-permute-done.refs_1_ = f32[256,128]{1,0:T(8,128)S(1)} collective-permute-done((f32[256,128]{1,0:T(8,128)S(1)}, f32[256,128]{1,0:T(8,128)S(1)}, u32[]{:S(2)}, u32[]{:S(2)}) %collective-permute-start) | collective-permute-done | bytes 131104 | tf_op jit(solution)/shard_map/ppermute | solution.py:286
  49.8 11.1 %tile.1 = (f32[288,128]{1,0:T(8,128)}, f32[128,128]{1,0:T(8,128)S(1)}) custom-call(f32[256,128]{1,0:T(8,128)S(1)} %bitcast.16, f32[256,128]{1,0:T(8,128)S(1)} %collective-permute-done.refs_1_, f32[288,128]{1,0:T(8,128)S(1)} %get-tuple-element.22.refs_2_, bf16[2,288,512]{2,1,0:T(8,128)(2,1)S(1)} %get-tuple-element.23.refs_3_, s32[1]{0:T(128)} %bitcast.9.refs_4_), custom_call_target="tpu_custom_call" | custom-call | tf_op jit(solution)/shard_map/tile/pallas_call | solution.py:287
  60.9 10.9 %all_to_all.15 = f32[32,4,128]{2,1,0:T(4,128)S(1)} all-to-all(f32[32,4,128]{2,1,0:T(4,128)S(1)} %bitcast.22), channel_id=1, replica_groups=mesh['grp'=16,'place'=16,'core'=2] {'place','core'}, dimensions={0} | all-to-all | bytes 131072 | tf_op jit(solution)/shard_map/all_to_all | solution.py:293
  71.8 0.8 ungroup.1
  72.6 3.5 %all-to-all-start.2 = ((f32[16,8,128]{2,1,0:T(8,128)}), f32[16,8,128]{2,1,0:T(8,128)S(1)}, u32[]{:S(2)}, u32[]{:S(2)}) async-start(f32[16,8,128]{2,1,0:T(8,128)} %ungroup.1), calls=%async_computation.2 | async-start | bytes 131072 | tf_op jit(solution)/shard_map/all_to_all | solution.py:302
  76.8 0.0 copy-start.6
  76.8 1.5 %extra.1 = (f32[3,128]{1,0:T(4,128)}, f32[1,128]{1,0:T(1,128)}) custom-call(f32[288,128]{1,0:T(8,128)S(1)} %copy-done.4, s32[3,128]{1,0:T(4,128)S(1)} %copy-done.8, f32[3,128]{1,0:T(4,128)S(1)} %copy-done.9, f32[1,128]{1,0:T(1,128)S(1)} %bitcast.26, f32[288,512]{1,0:T(8,128)S(1)} %copy-done, f32[288,1]{1,0:T(8,128)S(1)} %reshape.48.iso_kernel_ref, ...), custom_call_target="tpu_custom_call" | custom-call | tf_op jit(solution)/shard_map/extra/pallas_call | solution.py:294
  78.3 9.5 %all-to-all-done.2.back_ref = f32[16,8,128]{2,1,0:T(8,128)S(1)} async-done(((f32[16,8,128]{2,1,0:T(8,128)}), f32[16,8,128]{2,1,0:T(8,128)S(1)}, u32[]{:S(2)}, u32[]{:S(2)}) %all-to-all-start.2) | async-done | bytes 65568 | tf_op jit(solution)/shard_map/all_to_all | solution.py:302
  87.8 1.4 %streams.1 = f32[8,128]{1,0:T(8,128)} custom-call(f32[16,8,128]{2,1,0:T(8,128)S(1)} %all-to-all-done.2.back_ref, f32[128,128]{1,0:T(8,128)S(1)} %get-tuple-element.26.length_ref, s32[128,128]{1,0:T(8,128)S(1)} %get-tuple-element.27.stream_ref, f32[8,128]{1,0:T(8,128)S(1)} %bitcast.24, f32[1]{0:T(128)S(6)} %copy.23.step_ref), custom_call_target="tpu_custom_call" | custom-call | tf_op jit(solution)/shard_map/streams/pallas_call | solution.py:303
  (15 shorter events, 0.0 us)
Async XLA Ops:
  0.6 29.5 %copy-start = (f32[288,512]{1,0:T(8,128)S(1)}, f32[288,512]{1,0:T(8,128)}, u32[]{:S(2)}) copy-start(f32[288,512]{1,0:T(8,128)} %kernel_ref.3) | copy-start | bytes 1769476
  3.0 25.5 %copy-start.2 = (s32[1,512,32]{1,2,0:T(8,128)S(1)}, s32[1,512,32]{1,2,0:T(8,128)}, u32[]{:S(2)}) copy-start(s32[1,512,32]{1,2,0:T(8,128)} %param.14) | copy-start | bytes 196612
  3.0 25.5 %copy-start.7 = (s32[1,512]{1,0:T(1,128)S(1)}, s32[1,512]{1,0:T(1,128)}, u32[]{:S(2)}) copy-start(s32[1,512]{1,0:T(1,128)} %refs_2_.1) | copy-start | bytes 6148
  3.0 40.5 %all-to-all-start = ((f32[256,1,128]{2,1,0:T(1,128)}), f32[256,1,128]{2,1,0:T(1,128)S(1)}, u32[]{:S(2)}, u32[]{:S(2)}) async-start(f32[256,1,128]{2,1,0:T(1,128)} %bitcast.6), calls=%async_computation | async-start | bytes 262144 | tf_op jit(solution)/shard_map/all_to_all | solution.py:274
  28.5 0.8 copy-start.3
  29.3 0.7 copy-start.11
  30.0 0.9 copy-start.5
  30.0 0.9 copy-start.8
  30.0 0.9 copy-start.9
  30.1 0.8 copy-start.10
  30.9 1.1 %copy-start.1 = (f32[288,512]{1,0:T(8,128)S(1)}, f32[288,512]{1,0:T(8,128)}, u32[]{:S(2)}) copy-start(f32[288,512]{1,0:T(8,128)} %intra_ref.1) | copy-start | bytes 1769476
  43.5 6.3 %collective-permute-start = (f32[256,128]{1,0:T(8,128)S(1)}, f32[256,128]{1,0:T(8,128)S(1)}, u32[]{:S(2)}, u32[]{:S(2)}) collective-permute-start(f32[256,128]{1,0:T(8,128)S(1)} %bitcast.15), channel_id=1, source_target_pairs={{0,1},{1,0},{2,3},{3,2},{4,5},{5,4},{6,7},{7,6},{8,9},{9,8},{10,11... | collective-permute-start | bytes 393224 | tf_op jit(solution)/shard_map/ppermute | solution.py:286
  71.8 5.0 %copy-start.4 = (f32[288,128]{1,0:T(8,128)S(1)}, f32[288,128]{1,0:T(8,128)}, u32[]{:S(2)}) copy-start(f32[288,128]{1,0:T(8,128)} %get-tuple-element.13.residual_ref) | copy-start | bytes 442372
  72.6 15.1 %all-to-all-start.2 = ((f32[16,8,128]{2,1,0:T(8,128)}), f32[16,8,128]{2,1,0:T(8,128)S(1)}, u32[]{:S(2)}, u32[]{:S(2)}) async-start(f32[16,8,128]{2,1,0:T(8,128)} %ungroup.1), calls=%async_computation.2 | async-start | bytes 131072 | tf_op jit(solution)/shard_map/all_to_all | solution.py:302
  76.8 11.0 %copy-start.6 = (f32[1024]{0:T(1024)S(1)}, f32[1024]{0:T(1024)}, u32[]{:S(2)}) copy-start(f32[1024]{0:T(1024)} %param.19) | copy-start | bytes 12292

commit v3 on v2

--- a/solution.py
+++ b/solution.py
@@ -7,7 +7,6 @@
 
 LANES = 128
 CORES = 2
-CHUNK = 64
 F32 = jnp.float32
 BF16 = jnp.bfloat16
 I16 = jnp.int16
@@ -110,43 +109,47 @@
     parts_ref[0], parts_ref[1] = split2(intra_ref[...])
 
 
-def tile_kernel(own_ref, other_ref, backdrop_ref, parts_ref, core_ref, residual_ref, back_ref,
-                value_ref, key_ref, found_ref, *, num_voxels, block, group_rows):
-    chips = own_ref.shape[0]
-    num_bins = parts_ref.shape[2]
+def unpack(ref, core, block):
+    mine = ref[...]
+    mine = jnp.where(core == 0, mine, pltpu.roll(mine, LANES // CORES, axis=1))
     per_row = LANES // block
-    rows = chips // per_row
-    places = rows // group_rows
-    chunks, chunk = key_ref.shape[:2]
+    rows = mine.shape[0] // per_row
+    quarters = [mine[b * rows:(b + 1) * rows, :] for b in range(per_row)]
+    return side_by_side(quarters, block), side_by_side(quarters, block, block).astype(jnp.int32)
+
+
+def where_bin(bin_ids, key_row, num_voxels):
+    return jnp.where(bin_ids == (key_row // num_voxels).astype(I16), jnp.ones((), BF16), jnp.zeros((), BF16))
+
+
+def scatter(value_ref, key_ref, num_bins, num_voxels):
+    zero = jnp.zeros((), BF16)
     bin_ids = iota((num_bins, LANES), 0).astype(I16)
     voxel_ids = iota((num_voxels, LANES), 0).astype(I16)
-    voxel_ids32 = iota((num_voxels, LANES), 0)
-    one, zero = jnp.ones((), BF16), jnp.zeros((), BF16)
-
-    for source, ref in enumerate((own_ref, other_ref)):
-        mine = ref[...]
-        mine = jnp.where(core_ref[0] == 0, mine, pltpu.roll(mine, LANES // CORES, axis=1))
-        quarters = [mine[b * rows:(b + 1) * rows, :] for b in range(per_row)]
-        value = side_by_side(quarters, block)
-        key = side_by_side(quarters, block, block)
-        for start in range(0, rows, chunk):
-            value_ref[(source * rows + start) // chunk] = value[start:start + chunk]
-            key_ref[(source * rows + start) // chunk] = key[start:start + chunk].astype(jnp.int32)
-
-    def hots(c):
-        return jnp.concatenate([
-            jnp.where(bin_ids == (key_ref[c, i:i + 1, :] // num_voxels).astype(I16), one, zero)
-            for i in range(chunk)], axis=1)
-
-    def scatter(c, acc):
-        spread = []
-        for i in range(chunk):
-            head, tail = split2(value_ref[c, i:i + 1, :])
-            here = voxel_ids == (key_ref[c, i:i + 1, :] % num_voxels).astype(I16)
-            spread.append(jnp.concatenate([jnp.where(here, head, zero), jnp.where(here, tail, zero)], axis=0))
-        return acc + dot(hots(c), jnp.concatenate(spread, axis=1), ((1,), (1,)))
-
-    acc = lax.fori_loop(0, chunks, scatter, jnp.zeros((num_bins, 2 * num_voxels), F32))
+    hots, spread = [], []
+    for n in range(key_ref.shape[0]):
+        key = key_ref[n:n + 1, :]
+        head, tail = split2(value_ref[n:n + 1, :])
+        here = voxel_ids == (key % num_voxels).astype(I16)
+        spread.append(jnp.concatenate([jnp.where(here, head, zero), jnp.where(here, tail, zero)], axis=0))
+        hots.append(where_bin(bin_ids, key, num_voxels))
+    return dot(jnp.concatenate(hots, axis=1), jnp.concatenate(spread, axis=1), ((1,), (1,)))
+
+
+def own_kernel(own_ref, acc_ref, keys_ref, value_ref, *, num_voxels, block):
+    value_ref[...], keys_ref[...] = unpack(own_ref, lax.axis_index("core"), block)
+    acc_ref[...] = scatter(value_ref, keys_ref, acc_ref.shape[0], num_voxels)
+
+
+def tile_kernel(other_ref, acc_ref, own_keys_ref, backdrop_ref, parts_ref, residual_ref, back_ref,
+                value_ref, keys_ref, found_ref, *, num_voxels, block, group_rows):
+    core = lax.axis_index("core")
+    num_bins = parts_ref.shape[2]
+    rows = keys_ref.shape[1]
+    places = rows // group_rows
+    keys_ref[0] = own_keys_ref[...]
+    value_ref[...], keys_ref[1] = unpack(other_ref, core, block)
+    acc = acc_ref[...] + scatter(value_ref, keys_ref.at[1], num_bins, num_voxels)
     fiber = jnp.concatenate(split2(acc[:, :num_voxels] + acc[:, num_voxels:]), axis=1)
     product = dot(parts_ref[0], fiber, ((1,), (0,))) + dot(parts_ref[1], fiber, ((1,), (0,)))
     residual = product[:, :num_voxels] + product[:, num_voxels:] + backdrop_ref[...]
@@ -154,23 +157,24 @@
     turned_residual = jnp.concatenate(split2(jnp.transpose(residual)), axis=0)
     product = dot(turned_residual, parts_ref[0], ((1,), (0,))) + dot(turned_residual, parts_ref[1], ((1,), (0,)))
     back = jnp.concatenate(split2(product[:num_voxels] + product[num_voxels:]), axis=0)
-
-    def gather(c, carry):
-        found = dot(back, hots(c), ((1,), (0,)))
+    bin_ids = iota((num_bins, LANES), 0).astype(I16)
+    voxel_ids = iota((num_voxels, LANES), 0)
+
+    def gather(source, carry):
+        hots = [where_bin(bin_ids, keys_ref[source, n:n + 1, :], num_voxels) for n in range(rows)]
+        found = dot(back, jnp.concatenate(hots, axis=1), ((1,), (0,)))
         found = found[:num_voxels] + found[num_voxels:]
-        for i in range(chunk):
-            hit = jnp.where(voxel_ids32 == key_ref[c, i:i + 1, :] % num_voxels,
-                            found[:, i * LANES:(i + 1) * LANES], 0.0)
-            found_ref[c, i:i + 1, :] = jnp.sum(hit, axis=0, keepdims=True)
+        for n in range(rows):
+            hit = jnp.where(voxel_ids == keys_ref[source, n:n + 1, :] % num_voxels,
+                            found[:, n * LANES:(n + 1) * LANES], 0.0)
+            found_ref[n:n + 1, :] = jnp.sum(hit, axis=0, keepdims=True)
+        source_core = jnp.where(source == 0, core, 1 - core)
+        for a in range(group_rows):
+            back_ref[pl.ds(source_core * group_rows + a, places, stride=CORES * group_rows), :] = (
+                found_ref[a * places:(a + 1) * places, :])
         return carry
 
-    lax.fori_loop(0, chunks, gather, 0)
-    for source in range(CORES):
-        source_core = core_ref[0] if source == 0 else 1 - core_ref[0]
-        for a in range(group_rows):
-            n = source * rows + a * places
-            back_ref[pl.ds(source_core * group_rows + a, places, stride=CORES * group_rows), :] = (
-                found_ref[n // chunk, n % chunk:n % chunk + places, :])
+    lax.fori_loop(0, CORES, gather, 0)
 
 
 def ungroup_kernel(in_ref, out_ref, *, block):
@@ -260,7 +264,6 @@
     weight_rows = stream_weight.reshape(num_streams // LANES, LANES)
     iso_row = iso_weight.reshape(1, num_voxels)
     iso_column = iso_kernel.reshape(num_dirs, 1)
-    core = lax.axis_index("core").astype(jnp.int32).reshape(1)
     by_slot = [jnp.swapaxes(x, 1, 2) for x in (seg_stream, seg_voxel, seg_bin, seg_length)]
 
     outgoing = call(
@@ -281,15 +284,21 @@
         backdrop_kernel, [shape((num_dirs, num_voxels)), shape((2, num_dirs, num_bins), BF16)],
         [VMEM] * 7, "backdrop",
     )(signal, peak_bin, extra_weight, iso_row, extra_kernel, iso_column, intra_kernel)
-    chunked = (rows // CHUNK, CHUNK, LANES)
     own, stream, length, backdrop, parts = lax.optimization_barrier((own, stream, length, backdrop, parts))
     other = lax.ppermute(own, "core", [(0, 1), (1, 0)])
+    own_rows = rows // CORES
+    acc, own_keys = call(
+        lambda *refs: own_kernel(*refs, num_voxels=num_voxels, block=block),
+        [shape((num_bins, 2 * num_voxels)), shape((own_rows, LANES), jnp.int32)], [VMEM], "own",
+        scratch=[pltpu.VMEM((own_rows, LANES), F32)], limit=24,
+    )(own)
     residual, seg_back = call(
         lambda *refs: tile_kernel(*refs, num_voxels=num_voxels, block=block, group_rows=group_rows),
-        [shape((num_dirs, num_voxels)), shape((rows, LANES))], [VMEM] * 4 + [SMEM], "tile",
-        scratch=[pltpu.VMEM(chunked, F32), pltpu.VMEM(chunked, jnp.int32), pltpu.VMEM(chunked, F32)],
+        [shape((num_dirs, num_voxels)), shape((rows, LANES))], [VMEM] * 5, "tile",
+        scratch=[pltpu.VMEM((own_rows, LANES), F32), pltpu.VMEM((CORES, own_rows, LANES), jnp.int32),
+                 pltpu.VMEM((own_rows, LANES), F32)],
         limit=32,
-    )(own, other, backdrop, parts, core)
+    )(other, acc, own_keys, backdrop, parts)
     returning = lax.all_to_all(seg_back.reshape(tiles, group_rows, LANES), ("place", "core"), split_axis=0, concat_axis=0, tiled=True)
     new_extra, new_iso = call(
         extra_kernel_body, [shape(extra_weight.shape), shape((1, num_voxels))],

time: 89.7 us -> 89.1 us (level)
  waiting for transfers between devices: 21.1 us -> 20.1 us
    pallas_call x0 -> x1, Pallas kernels: none -> 2.56 us  [on_device(): call(lambda *refs: own_kernel(*refs, num_voxels=num_voxels, block=block),...]
    pallas_call x1, Pallas kernels: 11.1 us -> 8.97 us  [on_device(): call(lambda *refs: tile_kernel(*refs, num_voxels=num_voxels, block=block,...]
    ppermute x1, waiting for transfers between devices: 0.96 us -> 0.01 us  [on_device(): other = lax.ppermute(own, 'core', [(0, 1), (1, 0)])]
  transfers between devices with their start and end apart: 3 -> 3, of which waited for: 3 -> 2; matrix products, arithmetic and copies ran while one was open for 0% -> 0% of each run, Pallas kernels for 3% -> 6%
where the time goes in v3:
time: 89.1 us; the launch traced here: 88.6 us
  starting transfers between devices  34.5 us (39%)
  waiting for transfers between devices  20.1 us (23%)
  Pallas kernels  18.7 us (21%)
  blocking collectives  10.7 us (12%)
  local copies, waits for them, and re-layouts  3.21 us (4%)
  between operations  1.44 us (2%)
    all_to_all x1, starting transfers between devices, on_device(): lax.all_to_all(outgoing.reshape(chips, 1, LANES), ('grp', 'place'), split...  25.5 us
    all_to_all x1, blocking collectives, on_device(): lax.all_to_all(seg_back.reshape(tiles, group_rows, LANES), ('place', 'cor...  10.7 us
    all_to_all x1, waiting for transfers between devices, on_device(): lax.all_to_all(outgoing.reshape(chips, 1, LANES), ('grp', 'place'), split...  10.7 us
    all_to_all x1, waiting for transfers between devices, on_device(): lax.all_to_all(ungrouped, 'grp', split_axis=0, concat_axis=0, tiled=True)  9.48 us
    pallas_call x1, Pallas kernels, on_device(): call(lambda *refs: tile_kernel(*refs, num_voxels=num_voxels, block=block,...  8.97 us
    ppermute x1, starting transfers between devices, on_device(): other = lax.ppermute(own, 'core', [(0, 1), (1, 0)])  5.52 us
    all_to_all x1, starting transfers between devices, on_device(): lax.all_to_all(ungrouped, 'grp', split_axis=0, concat_axis=0, tiled=True)  3.49 us
    unnamed x24, local copies, waits for them, and re-layouts  3.12 us
  transfers between devices with their start and end apart: 3, of which 2 were waited for; matrix products, arithmetic and copies ran while one was open for 0% of the time, Pallas kernels for 6%

profile of v3, /device:TPU:1, one launch (start us, length us, event | category | flops | bytes accessed | tf_op | source)
XLA Modules:
  0.0 88.6 jit_solution(13725305527856732494)
XLA Ops:
  0.6 2.3 %prepare.1 = f32[256,128]{1,0:T(8,128)} custom-call(s32[1,32,512]{2,1,0:T(8,128)} %bitcast.16, s32[1,32,512]{2,1,0:T(8,128)} %bitcast.26, s32[1,32,512]{2,1,0:T(8,128)} %bitcast.27, f32[1,32,512]{2,1,0:T(8,128)} %bitcast.18, s32[1,512]{1,0:T(1,128)} %refs_2_.1, f32[8,128]{1,0:T(8,128)} %bitcast.22), custom_call_target="tpu_custom_call" | custom-call | tf_op jit(solution)/shard_map/prepare/pallas_call | solution.py:269
  3.0 0.0 copy-start.2
  3.0 0.0 copy-start.7
  3.0 25.5 %all-to-all-start = ((f32[256,1,128]{2,1,0:T(1,128)}), f32[256,1,128]{2,1,0:T(1,128)S(1)}, u32[]{:S(2)}, u32[]{:S(2)}) async-start(f32[256,1,128]{2,1,0:T(1,128)} %bitcast.6), calls=%async_computation | async-start | bytes 262144 | tf_op jit(solution)/shard_map/all_to_all | solution.py:277
  28.5 0.0 copy-start.3
  28.5 0.8 copy-done.3
  29.3 0.3 slots.1
  29.6 0.4 copy-done.11
  30.0 0.1 reshape.44.iso_kernel_ref
  30.1 0.0 copy-start.10
  30.1 0.8 copy-done.5
  30.9 1.1 %copy-done.1 = f32[288,512]{1,0:T(8,128)S(1)} copy-done((f32[288,512]{1,0:T(8,128)S(1)}, f32[288,512]{1,0:T(8,128)}, u32[]{:S(2)}) %copy-start.1) | copy-done | bytes 589848
  32.0 0.8 backdrop.1
  32.8 10.7 %all-to-all-done = f32[256,1,128]{2,1,0:T(1,128)S(1)} async-done(((f32[256,1,128]{2,1,0:T(1,128)}), f32[256,1,128]{2,1,0:T(1,128)S(1)}, u32[]{:S(2)}, u32[]{:S(2)}) %all-to-all-start) | async-done | bytes 131104 | tf_op jit(solution)/shard_map/all_to_all | solution.py:277
  43.5 5.5 %collective-permute-start = (f32[256,128]{1,0:T(8,128)S(1)}, f32[256,128]{1,0:T(8,128)S(1)}, u32[]{:S(2)}, u32[]{:S(2)}) collective-permute-start(f32[256,128]{1,0:T(8,128)S(1)} %bitcast.14), channel_id=1, source_target_pairs={{0,1},{1,0},{2,3},{3,2},{4,5},{5,4},{6,7},{7,6},{8,9},{9,8},{10,11... | collective-permute-start | bytes 393224 | tf_op jit(solution)/shard_map/ppermute | solution.py:288
  49.0 2.6 %own.1 = (f32[512,256]{1,0:T(8,128)S(1)}, s32[64,128]{1,0:T(8,128)S(1)}) custom-call(f32[256,128]{1,0:T(8,128)S(1)} %bitcast.15), custom_call_target="tpu_custom_call" | custom-call | tf_op jit(solution)/shard_map/own/pallas_call | solution.py:290
  51.6 9.0 %tile.1 = (f32[288,128]{1,0:T(8,128)}, f32[128,128]{1,0:T(8,128)S(1)}) custom-call(f32[256,128]{1,0:T(8,128)S(1)} %collective-permute-done.refs_0_, f32[512,256]{1,0:T(8,128)S(1)} %get-tuple-element.24.refs_1_, s32[64,128]{1,0:T(8,128)S(1)} %get-tuple-element.25.refs_2_, f32[288,128]{1,0:T(8,128)S(1)} %get-tuple-element.26.refs_3_, ...), custom_call_target="tpu_custom_call" | custom-call | tf_op jit(solution)/shard_map/tile/pallas_call | solution.py:295
  60.5 10.7 %all_to_all.15 = f32[32,4,128]{2,1,0:T(4,128)S(1)} all-to-all(f32[32,4,128]{2,1,0:T(4,128)S(1)} %bitcast.21), channel_id=1, replica_groups=mesh['grp'=16,'place'=16,'core'=2] {'place','core'}, dimensions={0} | all-to-all | bytes 131072 | tf_op jit(solution)/shard_map/all_to_all | solution.py:302
  71.2 0.8 ungroup.1
  72.1 3.5 %all-to-all-start.2 = ((f32[16,8,128]{2,1,0:T(8,128)}), f32[16,8,128]{2,1,0:T(8,128)S(1)}, u32[]{:S(2)}, u32[]{:S(2)}) async-start(f32[16,8,128]{2,1,0:T(8,128)} %ungroup.1), calls=%async_computation.2 | async-start | bytes 131072 | tf_op jit(solution)/shard_map/all_to_all | solution.py:311
  76.2 0.0 copy-start.6
  76.2 1.5 %extra.1 = (f32[3,128]{1,0:T(4,128)}, f32[1,128]{1,0:T(1,128)}) custom-call(f32[288,128]{1,0:T(8,128)S(1)} %copy-done.4, s32[3,128]{1,0:T(4,128)S(1)} %copy-done.8, f32[3,128]{1,0:T(4,128)S(1)} %copy-done.9, f32[1,128]{1,0:T(1,128)S(1)} %bitcast.25, f32[288,512]{1,0:T(8,128)S(1)} %copy-done, f32[288,1]{1,0:T(8,128)S(1)} %reshape.44.iso_kernel_ref, ...), custom_call_target="tpu_custom_call" | custom-call | tf_op jit(solution)/shard_map/extra/pallas_call | solution.py:303
  77.7 9.5 %all-to-all-done.2.back_ref = f32[16,8,128]{2,1,0:T(8,128)S(1)} async-done(((f32[16,8,128]{2,1,0:T(8,128)}), f32[16,8,128]{2,1,0:T(8,128)S(1)}, u32[]{:S(2)}, u32[]{:S(2)}) %all-to-all-start.2) | async-done | bytes 65568 | tf_op jit(solution)/shard_map/all_to_all | solution.py:311
  87.2 1.4 %streams.1 = f32[8,128]{1,0:T(8,128)} custom-call(f32[16,8,128]{2,1,0:T(8,128)S(1)} %all-to-all-done.2.back_ref, f32[128,128]{1,0:T(8,128)S(1)} %get-tuple-element.30.length_ref, s32[128,128]{1,0:T(8,128)S(1)} %get-tuple-element.31.stream_ref, f32[8,128]{1,0:T(8,128)S(1)} %bitcast.23, f32[1]{0:T(128)S(6)} %copy.23.step_ref), custom_call_target="tpu_custom_call" | custom-call | tf_op jit(solution)/shard_map/streams/pallas_call | solution.py:312
  (16 shorter events, 0.0 us)
Async XLA Ops:
  0.6 29.5 %copy-start = (f32[288,512]{1,0:T(8,128)S(1)}, f32[288,512]{1,0:T(8,128)}, u32[]{:S(2)}) copy-start(f32[288,512]{1,0:T(8,128)} %kernel_ref.3) | copy-start | bytes 1769476
  3.0 25.5 %copy-start.2 = (s32[1,512,32]{1,2,0:T(8,128)S(1)}, s32[1,512,32]{1,2,0:T(8,128)}, u32[]{:S(2)}) copy-start(s32[1,512,32]{1,2,0:T(8,128)} %param.14) | copy-start | bytes 196612
  3.0 25.5 %copy-start.7 = (s32[1,512]{1,0:T(1,128)S(1)}, s32[1,512]{1,0:T(1,128)}, u32[]{:S(2)}) copy-start(s32[1,512]{1,0:T(1,128)} %refs_2_.1) | copy-start | bytes 6148
  3.0 40.5 %all-to-all-start = ((f32[256,1,128]{2,1,0:T(1,128)}), f32[256,1,128]{2,1,0:T(1,128)S(1)}, u32[]{:S(2)}, u32[]{:S(2)}) async-start(f32[256,1,128]{2,1,0:T(1,128)} %bitcast.6), calls=%async_computation | async-start | bytes 262144 | tf_op jit(solution)/shard_map/all_to_all | solution.py:277
  28.5 0.8 copy-start.3
  29.3 0.7 copy-start.11
  30.0 0.9 copy-start.5
  30.0 0.9 copy-start.8
  30.0 0.9 copy-start.9
  30.1 0.8 copy-start.10
  30.9 1.1 %copy-start.1 = (f32[288,512]{1,0:T(8,128)S(1)}, f32[288,512]{1,0:T(8,128)}, u32[]{:S(2)}) copy-start(f32[288,512]{1,0:T(8,128)} %intra_ref.1) | copy-start | bytes 1769476
  43.5 8.1 %collective-permute-start = (f32[256,128]{1,0:T(8,128)S(1)}, f32[256,128]{1,0:T(8,128)S(1)}, u32[]{:S(2)}, u32[]{:S(2)}) collective-permute-start(f32[256,128]{1,0:T(8,128)S(1)} %bitcast.14), channel_id=1, source_target_pairs={{0,1},{1,0},{2,3},{3,2},{4,5},{5,4},{6,7},{7,6},{8,9},{9,8},{10,11... | collective-permute-start | bytes 393224 | tf_op jit(solution)/shard_map/ppermute | solution.py:288
  71.2 5.0 %copy-start.4 = (f32[288,128]{1,0:T(8,128)S(1)}, f32[288,128]{1,0:T(8,128)}, u32[]{:S(2)}) copy-start(f32[288,128]{1,0:T(8,128)} %get-tuple-element.15.residual_ref) | copy-start | bytes 442372
  72.1 15.1 %all-to-all-start.2 = ((f32[16,8,128]{2,1,0:T(8,128)}), f32[16,8,128]{2,1,0:T(8,128)S(1)}, u32[]{:S(2)}, u32[]{:S(2)}) async-start(f32[16,8,128]{2,1,0:T(8,128)} %ungroup.1), calls=%async_computation.2 | async-start | bytes 131072 | tf_op jit(solution)/shard_map/all_to_all | solution.py:311
  76.2 11.0 %copy-start.6 = (f32[1024]{0:T(1024)S(1)}, f32[1024]{0:T(1024)}, u32[]{:S(2)}) copy-start(f32[1024]{0:T(1024)} %param.19) | copy-start | bytes 12292

commit v4 on v3

--- a/solution.py
+++ b/solution.py
@@ -10,7 +10,6 @@
 F32 = jnp.float32
 BF16 = jnp.bfloat16
 I16 = jnp.int16
-HIGH = lax.Precision.HIGHEST
 
 
 def iota(shape, dim):
@@ -97,15 +96,21 @@
 
 
 def backdrop_kernel(signal_ref, peak_ref, extra_ref, iso_ref, kernel_ref, iso_kernel_ref, intra_ref,
-                    out_ref, parts_ref):
+                    out_ref, parts_ref, peak_kernel_ref):
     num_bins = kernel_ref.shape[1]
     num_voxels = peak_ref.shape[1]
+    peaks = peak_ref.shape[0]
     bins = iota((num_bins, num_voxels), 0)
-    extra_map = jnp.zeros((num_bins, num_voxels), F32)
-    for k in range(peak_ref.shape[0]):
-        extra_map += jnp.where(bins == peak_ref[k:k + 1, :], extra_ref[k:k + 1, :], 0.0)
-    zeppelin = jnp.dot(kernel_ref[...], extra_map, precision=HIGH, preferred_element_type=F32)
-    out_ref[...] = zeppelin + iso_kernel_ref[...] * iso_ref[...] - signal_ref[...].astype(F32)
+    hot = jnp.concatenate([(bins == peak_ref[k:k + 1, :]).astype(F32).astype(BF16) for k in range(peaks)], axis=1)
+    head, rest = kernel_ref[...].astype(BF16), kernel_ref[...]
+    middle, tail = split2(rest - head.astype(F32))
+    columns = dot(head, hot, ((1,), (0,))) + dot(middle, hot, ((1,), (0,))) + dot(tail, hot, ((1,), (0,)))
+    backdrop = iso_kernel_ref[...] * iso_ref[...] - signal_ref[...].astype(F32)
+    for k in range(peaks):
+        column = columns[:, k * num_voxels:(k + 1) * num_voxels]
+        peak_kernel_ref[k] = column
+        backdrop += column * extra_ref[k:k + 1, :]
+    out_ref[...] = backdrop
     parts_ref[0], parts_ref[1] = split2(intra_ref[...])
 
 
@@ -141,7 +146,9 @@
     acc_ref[...] = scatter(value_ref, keys_ref, acc_ref.shape[0], num_voxels)
 
 
-def tile_kernel(other_ref, acc_ref, own_keys_ref, backdrop_ref, parts_ref, residual_ref, back_ref,
+def tile_kernel(other_ref, acc_ref, own_keys_ref, backdrop_ref, parts_ref, peak_kernel_ref, extra_ref,
+                iso_ref, iso_kernel_ref, step_ref,
+                residual_ref, back_ref, new_extra_ref, new_iso_ref,
                 value_ref, keys_ref, found_ref, *, num_voxels, block, group_rows):
     core = lax.axis_index("core")
     num_bins = parts_ref.shape[2]
@@ -157,6 +164,14 @@
     turned_residual = jnp.concatenate(split2(jnp.transpose(residual)), axis=0)
     product = dot(turned_residual, parts_ref[0], ((1,), (0,))) + dot(turned_residual, parts_ref[1], ((1,), (0,)))
     back = jnp.concatenate(split2(product[:num_voxels] + product[num_voxels:]), axis=0)
+
+    step = step_ref[0]
+    for k in range(peak_kernel_ref.shape[0]):
+        grad = jnp.sum(peak_kernel_ref[k] * residual, axis=0, keepdims=True)
+        new_extra_ref[k:k + 1, :] = jnp.maximum(extra_ref[k:k + 1, :] - step * grad, 0.0)
+    grad = jnp.sum(iso_kernel_ref[...] * residual, axis=0, keepdims=True)
+    new_iso_ref[...] = jnp.maximum(iso_ref[...] - step * grad, 0.0)
+
     bin_ids = iota((num_bins, LANES), 0).astype(I16)
     voxel_ids = iota((num_voxels, LANES), 0)
 
@@ -186,22 +201,6 @@
                  for u in range(per_row)]
         for b in range(per_row):
             out_ref[b * group_rows + a] = side_by_side([roll(part, -block * b) for part in parts], block)
-
-
-def extra_kernel_body(residual_ref, peak_ref, extra_ref, iso_ref, kernel_ref, iso_kernel_ref, step_ref,
-                      new_extra_ref, new_iso_ref):
-    num_bins = kernel_ref.shape[1]
-    num_voxels = peak_ref.shape[1]
-    step = step_ref[0]
-    residual = residual_ref[...]
-    back = lax.dot_general(kernel_ref[...], residual, (((0,), (0,)), ((), ())),
-                           precision=HIGH, preferred_element_type=F32)
-    bins = iota((num_bins, num_voxels), 0)
-    for k in range(peak_ref.shape[0]):
-        grad = jnp.sum(jnp.where(bins == peak_ref[k:k + 1, :], back, 0.0), axis=0, keepdims=True)
-        new_extra_ref[k:k + 1, :] = jnp.maximum(extra_ref[k:k + 1, :] - step * grad, 0.0)
-    grad = jnp.sum(iso_kernel_ref[...] * residual, axis=0, keepdims=True)
-    new_iso_ref[...] = jnp.maximum(iso_ref[...] - step * grad, 0.0)
 
 
 def stream_kernel(back_ref, length_ref, stream_ref, weight_ref, step_ref, out_ref):
@@ -280,11 +279,13 @@
         lambda *refs: slots_kernel(*refs, tiles=tiles),
         [shape((rows, LANES), jnp.int32), shape((rows, LANES))], [VMEM] * 3, "slots",
     )(by_slot[0], by_slot[3], seg_count)
-    backdrop, parts = call(
-        backdrop_kernel, [shape((num_dirs, num_voxels)), shape((2, num_dirs, num_bins), BF16)],
+    backdrop, parts, peak_kernel = call(
+        backdrop_kernel,
+        [shape((num_dirs, num_voxels)), shape((2, num_dirs, num_bins), BF16), shape((*peak_bin.shape[:1], num_dirs, num_voxels))],
         [VMEM] * 7, "backdrop",
     )(signal, peak_bin, extra_weight, iso_row, extra_kernel, iso_column, intra_kernel)
-    own, stream, length, backdrop, parts = lax.optimization_barrier((own, stream, length, backdrop, parts))
+    own, stream, length, backdrop, parts, peak_kernel = lax.optimization_barrier(
+        (own, stream, length, backdrop, parts, peak_kernel))
     other = lax.ppermute(own, "core", [(0, 1), (1, 0)])
     own_rows = rows // CORES
     acc, own_keys = call(
@@ -292,18 +293,15 @@
         [shape((num_bins, 2 * num_voxels)), shape((own_rows, LANES), jnp.int32)], [VMEM], "own",
         scratch=[pltpu.VMEM((own_rows, LANES), F32)], limit=24,
     )(own)
-    residual, seg_back = call(
+    residual, seg_back, new_extra, new_iso = call(
         lambda *refs: tile_kernel(*refs, num_voxels=num_voxels, block=block, group_rows=group_rows),
-        [shape((num_dirs, num_voxels)), shape((rows, LANES))], [VMEM] * 5, "tile",
+        [shape((num_dirs, num_voxels)), shape((rows, LANES)), shape(extra_weight.shape), shape((1, num_voxels))],
+        [VMEM] * 9 + [SMEM], "tile",
         scratch=[pltpu.VMEM((own_rows, LANES), F32), pltpu.VMEM((CORES, own_rows, LANES), jnp.int32),
                  pltpu.VMEM((own_rows, LANES), F32)],
         limit=32,
-    )(other, acc, own_keys, backdrop, parts)
+    )(other, acc, own_keys, backdrop, parts, peak_kernel, extra_weight, iso_row, iso_column, step_size)
     returning = lax.all_to_all(seg_back.reshape(tiles, group_rows, LANES), ("place", "core"), split_axis=0, concat_axis=0, tiled=True)
-    new_extra, new_iso = call(
-        extra_kernel_body, [shape(extra_weight.shape), shape((1, num_voxels))],
-        [VMEM] * 6 + [SMEM], "extra",
-    )(residual, peak_bin, extra_weight, iso_row, extra_kernel, iso_column, step_size)
     ungrouped = call(
         lambda *refs: ungroup_kernel(*refs, block=block),
         shape((groups, tile_rows, LANES)), [VMEM], "ungroup",

time: 89.1 us -> 88.3 us (level)
  blocking collectives: 10.7 us -> 25 us
  waiting for transfers between devices: 20.1 us -> 10.7 us
  starting transfers between devices: 34.5 us -> 31 us
  Pallas kernels: 18.7 us -> 16.5 us
    all_to_all x0 -> x1, blocking collectives: none -> 14.3 us  [on_device(): lax.all_to_all(ungrouped, 'grp', split_axis=0, concat_axis=0, tiled=True)]
    all_to_all x1 -> x0, waiting for transfers between devices: 9.48 us -> none  [on_device(): lax.all_to_all(ungrouped, 'grp', split_axis=0, concat_axis=0, tiled=True)]
    all_to_all x1 -> x0, starting transfers between devices: 3.49 us -> none  [on_device(): lax.all_to_all(ungrouped, 'grp', split_axis=0, concat_axis=0, tiled=True)]
    pallas_call x1 -> x0, Pallas kernels: 1.49 us -> none  [on_device(): call(extra_kernel_body, [shape(extra_weight.shape), shape((1, num_voxels)...]
    unnamed x24 -> x22, local copies, waits for them, and re-layouts: 3.12 us -> 3.11 us
  transfers between devices with their start and end apart: 3 -> 2, of which waited for: 2 -> 1; matrix products, arithmetic and copies ran while one was open for 0% -> 0% of each run, Pallas kernels for 6% -> 4%
where the time goes in v4:
time: 88.3 us; the launch traced here: 87.8 us
  starting transfers between devices  31 us (35%)
  blocking collectives  25 us (28%)
  Pallas kernels  16.5 us (19%)
  waiting for transfers between devices  10.7 us (12%)
  local copies, waits for them, and re-layouts  3.2 us (4%)
  between operations  1.43 us (2%)
    all_to_all x1, starting transfers between devices, on_device(): lax.all_to_all(outgoing.reshape(chips, 1, LANES), ('grp', 'place'), split...  25.5 us
    all_to_all x1, blocking collectives, on_device(): lax.all_to_all(ungrouped, 'grp', split_axis=0, concat_axis=0, tiled=True)  14.3 us
    all_to_all x1, waiting for transfers between devices, on_device(): lax.all_to_all(outgoing.reshape(chips, 1, LANES), ('grp', 'place'), split...  10.7 us
    all_to_all x1, blocking collectives, on_device(): lax.all_to_all(seg_back.reshape(tiles, group_rows, LANES), ('place', 'cor...  10.7 us
    pallas_call x1, Pallas kernels, on_device(): call(lambda *refs: tile_kernel(*refs, num_voxels=num_voxels, block=block,...  9 us
    ppermute x1, starting transfers between devices, on_device(): other = lax.ppermute(own, 'core', [(0, 1), (1, 0)])  5.52 us
    unnamed x22, local copies, waits for them, and re-layouts  3.11 us
    pallas_call x1, Pallas kernels, on_device(): call(lambda *refs: own_kernel(*refs, num_voxels=num_voxels, block=block),...  2.56 us
  transfers between devices with their start and end apart: 2, of which 1 were waited for; matrix products, arithmetic and copies ran while one was open for 0% of the time, Pallas kernels for 4%

profile of v4, /device:TPU:1, one launch (start us, length us, event | category | flops | bytes accessed | tf_op | source)
XLA Modules:
  0.0 87.8 jit_solution(1782550209373314706)
XLA Ops:
  0.6 2.3 %prepare.1 = f32[256,128]{1,0:T(8,128)} custom-call(s32[1,32,512]{2,1,0:T(8,128)} %bitcast.16, s32[1,32,512]{2,1,0:T(8,128)} %bitcast.26, s32[1,32,512]{2,1,0:T(8,128)} %bitcast.27, f32[1,32,512]{2,1,0:T(8,128)} %bitcast.18, s32[1,512]{1,0:T(1,128)} %refs_2_.1, f32[8,128]{1,0:T(8,128)} %bitcast.22), custom_call_target="tpu_custom_call" | custom-call | tf_op jit(solution)/shard_map/prepare/pallas_call | solution.py:268
  3.0 0.0 copy-start.2
  3.0 0.0 copy-start.6
  3.0 25.5 %all-to-all-start = ((f32[256,1,128]{2,1,0:T(1,128)}), f32[256,1,128]{2,1,0:T(1,128)S(1)}, u32[]{:S(2)}, u32[]{:S(2)}) async-start(f32[256,1,128]{2,1,0:T(1,128)} %bitcast.6), calls=%async_computation | async-start | bytes 262144 | tf_op jit(solution)/shard_map/all_to_all | solution.py:276
  28.5 0.0 copy-start.3
  28.5 0.8 copy-done.3
  29.3 0.3 slots.1
  29.6 0.4 copy-done.10
  30.0 0.1 reshape.44.iso_kernel_ref.refs_8_
  30.1 0.0 copy-start.8
  30.1 0.8 copy-done.4
  30.9 0.0 copy-done.9
  30.9 1.1 %copy-done.1 = f32[288,512]{1,0:T(8,128)S(1)} copy-done((f32[288,512]{1,0:T(8,128)S(1)}, f32[288,512]{1,0:T(8,128)}, u32[]{:S(2)}) %copy-start.1) | copy-done | bytes 589848
  32.0 0.8 backdrop.1
  32.7 10.7 %all-to-all-done = f32[256,1,128]{2,1,0:T(1,128)S(1)} async-done(((f32[256,1,128]{2,1,0:T(1,128)}), f32[256,1,128]{2,1,0:T(1,128)S(1)}, u32[]{:S(2)}, u32[]{:S(2)}) %all-to-all-start) | async-done | bytes 131104 | tf_op jit(solution)/shard_map/all_to_all | solution.py:276
  43.5 5.5 %collective-permute-start = (f32[256,128]{1,0:T(8,128)S(1)}, f32[256,128]{1,0:T(8,128)S(1)}, u32[]{:S(2)}, u32[]{:S(2)}) collective-permute-start(f32[256,128]{1,0:T(8,128)S(1)} %bitcast.14), channel_id=1, source_target_pairs={{0,1},{1,0},{2,3},{3,2},{4,5},{5,4},{6,7},{7,6},{8,9},{9,8},{10,11... | collective-permute-start | bytes 393224 | tf_op jit(solution)/shard_map/ppermute | solution.py:289
  49.6 2.6 %own.1 = (f32[512,256]{1,0:T(8,128)S(1)}, s32[64,128]{1,0:T(8,128)S(1)}) custom-call(f32[256,128]{1,0:T(8,128)S(1)} %bitcast.15), custom_call_target="tpu_custom_call" | custom-call | tf_op jit(solution)/shard_map/own/pallas_call | solution.py:291
  52.2 0.0 collective-permute-done.refs_0_
  52.2 9.0 %tile.1 = (f32[288,128]{1,0:T(8,128)}, f32[128,128]{1,0:T(8,128)S(1)}, f32[3,128]{1,0:T(4,128)}, f32[1,128]{1,0:T(1,128)}) custom-call(f32[256,128]{1,0:T(8,128)S(1)} %collective-permute-done.refs_0_, f32[512,256]{1,0:T(8,128)S(1)} %get-tuple-element.27.refs_1_, s32[64,128]{1,0:T(8,128)S(1)} %get-tuple-element.28.refs_2_, ...), custom_call_target="tpu_custom_call" | custom-call | tf_op jit(solution)/shard_map/tile/pallas_call | solution.py:296
  61.2 10.7 %all_to_all.15 = f32[32,4,128]{2,1,0:T(4,128)S(1)} all-to-all(f32[32,4,128]{2,1,0:T(4,128)S(1)} %bitcast.21), channel_id=1, replica_groups=mesh['grp'=16,'place'=16,'core'=2] {'place','core'}, dimensions={0} | all-to-all | bytes 131072 | tf_op jit(solution)/shard_map/all_to_all | solution.py:304
  71.9 0.2 ungroup.1
  72.1 0.0 copy-start.5
  72.1 14.3 %all_to_all.16.back_ref = f32[16,8,128]{2,1,0:T(8,128)S(1)} all-to-all(f32[16,8,128]{2,1,0:T(8,128)S(1)} %ungroup.1), channel_id=1, replica_groups=mesh['grp'=16,'place'=16,'core'=2] {'grp'}, dimensions={0} | all-to-all | bytes 131072 | tf_op jit(solution)/shard_map/all_to_all | solution.py:309
  86.4 1.4 %streams.1 = f32[8,128]{1,0:T(8,128)} custom-call(f32[16,8,128]{2,1,0:T(8,128)S(1)} %all_to_all.16.back_ref, f32[128,128]{1,0:T(8,128)S(1)} %get-tuple-element.34.length_ref, s32[128,128]{1,0:T(8,128)S(1)} %get-tuple-element.35.stream_ref, f32[8,128]{1,0:T(8,128)S(1)} %bitcast.23, f32[1]{0:T(128)S(6)} %copy.23.refs_9_.step_ref), custom_call_target="tpu_custom_call" | custom-call | tf_op jit(solution)/shard_map/streams/pallas_call | solution.py:310
  (12 shorter events, 0.0 us)
Async XLA Ops:
  0.6 29.5 %copy-start = (f32[288,512]{1,0:T(8,128)S(1)}, f32[288,512]{1,0:T(8,128)}, u32[]{:S(2)}) copy-start(f32[288,512]{1,0:T(8,128)} %kernel_ref.1) | copy-start | bytes 1769476
  3.0 25.5 %copy-start.2 = (s32[1,512,32]{1,2,0:T(8,128)S(1)}, s32[1,512,32]{1,2,0:T(8,128)}, u32[]{:S(2)}) copy-start(s32[1,512,32]{1,2,0:T(8,128)} %param.14) | copy-start | bytes 196612
  3.0 25.5 %copy-start.6 = (s32[1,512]{1,0:T(1,128)S(1)}, s32[1,512]{1,0:T(1,128)}, u32[]{:S(2)}) copy-start(s32[1,512]{1,0:T(1,128)} %refs_2_.1) | copy-start | bytes 6148
  3.0 40.5 %all-to-all-start = ((f32[256,1,128]{2,1,0:T(1,128)}), f32[256,1,128]{2,1,0:T(1,128)S(1)}, u32[]{:S(2)}, u32[]{:S(2)}) async-start(f32[256,1,128]{2,1,0:T(1,128)} %bitcast.6), calls=%async_computation | async-start | bytes 262144 | tf_op jit(solution)/shard_map/all_to_all | solution.py:276
  28.5 0.8 copy-start.3
  29.3 0.7 copy-start.10
  30.0 0.9 %copy-start.4 = (bf16[288,128]{1,0:T(8,128)(2,1)S(1)}, bf16[288,128]{1,0:T(8,128)(2,1)}, u32[]{:S(2)}) copy-start(bf16[288,128]{1,0:T(8,128)(2,1)} %signal_ref.1) | copy-start | bytes 221188
  30.0 0.9 %copy-start.7 = (f32[3,128]{1,0:T(4,128)S(1)}, f32[3,128]{1,0:T(4,128)}, u32[]{:S(2)}) copy-start(f32[3,128]{1,0:T(4,128)} %refs_6_.1) | copy-start | bytes 4612
  30.0 0.9 %copy-start.9 = (s32[3,128]{1,0:T(4,128)S(1)}, s32[3,128]{1,0:T(4,128)}, u32[]{:S(2)}) copy-start(s32[3,128]{1,0:T(4,128)} %peak_ref.1) | copy-start | bytes 4612
  30.1 0.8 copy-start.8
  30.9 1.1 %copy-start.1 = (f32[288,512]{1,0:T(8,128)S(1)}, f32[288,512]{1,0:T(8,128)}, u32[]{:S(2)}) copy-start(f32[288,512]{1,0:T(8,128)} %intra_ref.1) | copy-start | bytes 1769476
  43.5 8.7 %collective-permute-start = (f32[256,128]{1,0:T(8,128)S(1)}, f32[256,128]{1,0:T(8,128)S(1)}, u32[]{:S(2)}, u32[]{:S(2)}) collective-permute-start(f32[256,128]{1,0:T(8,128)S(1)} %bitcast.14), channel_id=1, source_target_pairs={{0,1},{1,0},{2,3},{3,2},{4,5},{5,4},{6,7},{7,6},{8,9},{9,8},{10,11... | collective-permute-start | bytes 393224 | tf_op jit(solution)/shard_map/ppermute | solution.py:289
  72.1 14.3 %copy-start.5 = (f32[1024]{0:T(1024)S(1)}, f32[1024]{0:T(1024)}, u32[]{:S(2)}) copy-start(f32[1024]{0:T(1024)} %param.19) | copy-start | bytes 12292

commit v5 on v4

--- a/solution.py
+++ b/solution.py
@@ -96,7 +96,7 @@
 
 
 def backdrop_kernel(signal_ref, peak_ref, extra_ref, iso_ref, kernel_ref, iso_kernel_ref, intra_ref,
-                    out_ref, parts_ref, peak_kernel_ref):
+                    step_ref, out_ref, parts_ref, peak_kernel_ref, step_row_ref):
     num_bins = kernel_ref.shape[1]
     num_voxels = peak_ref.shape[1]
     peaks = peak_ref.shape[0]
@@ -112,6 +112,7 @@
         backdrop += column * extra_ref[k:k + 1, :]
     out_ref[...] = backdrop
     parts_ref[0], parts_ref[1] = split2(intra_ref[...])
+    step_row_ref[...] = jnp.broadcast_to(step_ref[...], step_row_ref.shape)
 
 
 def unpack(ref, core, block):
@@ -165,7 +166,7 @@
     product = dot(turned_residual, parts_ref[0], ((1,), (0,))) + dot(turned_residual, parts_ref[1], ((1,), (0,)))
     back = jnp.concatenate(split2(product[:num_voxels] + product[num_voxels:]), axis=0)
 
-    step = step_ref[0]
+    step = step_ref[...]
     for k in range(peak_kernel_ref.shape[0]):
         grad = jnp.sum(peak_kernel_ref[k] * residual, axis=0, keepdims=True)
         new_extra_ref[k:k + 1, :] = jnp.maximum(extra_ref[k:k + 1, :] - step * grad, 0.0)
@@ -223,12 +224,11 @@
     lines = [jnp.concatenate([grad[per_row * r + q:per_row * r + q + 1, :] for q in range(per_row)], axis=1)
              for r in range(out_ref.shape[0])]
     grad = jnp.concatenate(lines, axis=0)
-    out_ref[...] = jnp.maximum(weight_ref[...] - step_ref[0] * grad, 0.0)
+    out_ref[...] = jnp.maximum(weight_ref[...] - step_ref[...] * grad, 0.0)
 
 
 VMEM = pl.BlockSpec(memory_space=pltpu.VMEM)
 HBM = pl.BlockSpec(memory_space=pltpu.HBM)
-SMEM = pl.BlockSpec(memory_space=pltpu.SMEM)
 
 
 def call(kernel, out_shape, in_specs, name, scratch=(), limit=16):
@@ -262,6 +262,7 @@
     group_rows = rows // tiles
     weight_rows = stream_weight.reshape(num_streams // LANES, LANES)
     iso_row = iso_weight.reshape(1, num_voxels)
+    step = step_size.reshape(1, 1)
     iso_column = iso_kernel.reshape(num_dirs, 1)
     by_slot = [jnp.swapaxes(x, 1, 2) for x in (seg_stream, seg_voxel, seg_bin, seg_length)]
 
@@ -279,13 +280,13 @@
         lambda *refs: slots_kernel(*refs, tiles=tiles),
         [shape((rows, LANES), jnp.int32), shape((rows, LANES))], [VMEM] * 3, "slots",
     )(by_slot[0], by_slot[3], seg_count)
-    backdrop, parts, peak_kernel = call(
+    backdrop, parts, peak_kernel, step_row = call(
         backdrop_kernel,
-        [shape((num_dirs, num_voxels)), shape((2, num_dirs, num_bins), BF16), shape((*peak_bin.shape[:1], num_dirs, num_voxels))],
-        [VMEM] * 7, "backdrop",
-    )(signal, peak_bin, extra_weight, iso_row, extra_kernel, iso_column, intra_kernel)
-    own, stream, length, backdrop, parts, peak_kernel = lax.optimization_barrier(
-        (own, stream, length, backdrop, parts, peak_kernel))
+        [shape((num_dirs, num_voxels)), shape((2, num_dirs, num_bins), BF16), shape((*peak_bin.shape[:1], num_dirs, num_voxels)), shape((1, LANES))],
+        [VMEM] * 8, "backdrop",
+    )(signal, peak_bin, extra_weight, iso_row, extra_kernel, iso_column, intra_kernel, step)
+    own, stream, length, backdrop, parts, peak_kernel, step_row = lax.optimization_barrier(
+        (own, stream, length, backdrop, parts, peak_kernel, step_row))
     other = lax.ppermute(own, "core", [(0, 1), (1, 0)])
     own_rows = rows // CORES
     acc, own_keys = call(
@@ -296,11 +297,11 @@
     residual, seg_back, new_extra, new_iso = call(
         lambda *refs: tile_kernel(*refs, num_voxels=num_voxels, block=block, group_rows=group_rows),
         [shape((num_dirs, num_voxels)), shape((rows, LANES)), shape(extra_weight.shape), shape((1, num_voxels))],
-        [VMEM] * 9 + [SMEM], "tile",
+        [VMEM] * 10, "tile",
         scratch=[pltpu.VMEM((own_rows, LANES), F32), pltpu.VMEM((CORES, own_rows, LANES), jnp.int32),
                  pltpu.VMEM((own_rows, LANES), F32)],
         limit=32,
-    )(other, acc, own_keys, backdrop, parts, peak_kernel, extra_weight, iso_row, iso_column, step_size)
+    )(other, acc, own_keys, backdrop, parts, peak_kernel, extra_weight, iso_row, iso_column, step_row)
     returning = lax.all_to_all(seg_back.reshape(tiles, group_rows, LANES), ("place", "core"), split_axis=0, concat_axis=0, tiled=True)
     ungrouped = call(
         lambda *refs: ungroup_kernel(*refs, block=block),
@@ -308,8 +309,8 @@
     )(returning.reshape(tiles * group_rows, LANES))
     returned = lax.all_to_all(ungrouped, "grp", split_axis=0, concat_axis=0, tiled=True)
     new_stream = call(
-        stream_kernel, shape(weight_rows.shape), [VMEM] * 4 + [SMEM], "streams",
-    )(returned, length, stream, weight_rows, step_size)
+        stream_kernel, shape(weight_rows.shape), [VMEM] * 5, "streams",
+    )(returned, length, stream, weight_rows, step_row)
     return (residual, new_stream.reshape(num_streams), new_extra, new_iso.reshape(num_voxels))
 
 

time: 88.3 us -> 87.7 us (level)
  no operation moved by 1% of the time
where the time goes in v5:
time: 87.7 us; the launch traced here: 87.2 us
  starting transfers between devices  31 us (35%)
  blocking collectives  25 us (29%)
  Pallas kernels  16.5 us (19%)
  waiting for transfers between devices  10.5 us (12%)
  local copies, waits for them, and re-layouts  2.77 us (3%)
  between operations  1.47 us (2%)
    all_to_all x1, starting transfers between devices, on_device(): lax.all_to_all(outgoing.reshape(chips, 1, LANES), ('grp', 'place'), split...  25.5 us
    all_to_all x1, blocking collectives, on_device(): lax.all_to_all(ungrouped, 'grp', split_axis=0, concat_axis=0, tiled=True)  14.3 us
    all_to_all x1, blocking collectives, on_device(): lax.all_to_all(seg_back.reshape(tiles, group_rows, LANES), ('place', 'cor...  10.7 us
    all_to_all x1, waiting for transfers between devices, on_device(): lax.all_to_all(outgoing.reshape(chips, 1, LANES), ('grp', 'place'), split...  10.5 us
    pallas_call x1, Pallas kernels, on_device(): call(lambda *refs: tile_kernel(*refs, num_voxels=num_voxels, block=block,...  9 us
    ppermute x1, starting transfers between devices, on_device(): other = lax.ppermute(own, 'core', [(0, 1), (1, 0)])  5.52 us
    unnamed x22, local copies, waits for them, and re-layouts  2.67 us
    pallas_call x1, Pallas kernels, on_device(): call(lambda *refs: own_kernel(*refs, num_voxels=num_voxels, block=block),...  2.56 us
  transfers between devices with their start and end apart: 2, of which 1 were waited for; matrix products, arithmetic and copies ran while one was open for 0% of the time, Pallas kernels for 4%

profile of v5, /device:TPU:1, one launch (start us, length us, event | category | flops | bytes accessed | tf_op | source)
XLA Modules:
  0.0 87.2 jit_solution(10867852519620220599)
XLA Ops:
  0.6 2.3 %prepare.1 = f32[256,128]{1,0:T(8,128)} custom-call(s32[1,32,512]{2,1,0:T(8,128)} %bitcast.18, s32[1,32,512]{2,1,0:T(8,128)} %bitcast.28, s32[1,32,512]{2,1,0:T(8,128)} %bitcast.29, f32[1,32,512]{2,1,0:T(8,128)} %bitcast.20, s32[1,512]{1,0:T(1,128)} %refs_2_.1, f32[8,128]{1,0:T(8,128)} %bitcast.24), custom_call_target="tpu_custom_call" | custom-call | tf_op jit(solution)/shard_map/prepare/pallas_call | solution.py:269
  3.0 0.0 copy-start.2
  3.0 0.0 copy-start.6
  3.0 25.5 %all-to-all-start = ((f32[256,1,128]{2,1,0:T(1,128)}), f32[256,1,128]{2,1,0:T(1,128)S(1)}, u32[]{:S(2)}, u32[]{:S(2)}) async-start(f32[256,1,128]{2,1,0:T(1,128)} %bitcast.6), calls=%async_computation | async-start | bytes 262144 | tf_op jit(solution)/shard_map/all_to_all | solution.py:277
  28.5 0.0 copy-start.3
  28.5 0.8 copy-done.3
  29.3 0.3 slots.1
  30.3 0.0 copy-start.4
  30.3 0.0 copy-start.8
  30.3 0.1 reshape.48.iso_kernel_ref.refs_8_
  30.4 0.0 copy-start.7
  30.4 0.0 copy-start.9
  30.4 0.7 copy-done.4
  31.2 1.1 %copy-done.1 = f32[288,512]{1,0:T(8,128)S(1)} copy-done((f32[288,512]{1,0:T(8,128)S(1)}, f32[288,512]{1,0:T(8,128)}, u32[]{:S(2)}) %copy-start.1) | copy-done | bytes 589848
  32.2 0.8 backdrop.1
  33.0 10.5 %all-to-all-done = f32[256,1,128]{2,1,0:T(1,128)S(1)} async-done(((f32[256,1,128]{2,1,0:T(1,128)}), f32[256,1,128]{2,1,0:T(1,128)S(1)}, u32[]{:S(2)}, u32[]{:S(2)}) %all-to-all-start) | async-done | bytes 131104 | tf_op jit(solution)/shard_map/all_to_all | solution.py:277
  43.5 5.5 %collective-permute-start = (f32[256,128]{1,0:T(8,128)S(1)}, f32[256,128]{1,0:T(8,128)S(1)}, u32[]{:S(2)}, u32[]{:S(2)}) collective-permute-start(f32[256,128]{1,0:T(8,128)S(1)} %bitcast.16), channel_id=1, source_target_pairs={{0,1},{1,0},{2,3},{3,2},{4,5},{5,4},{6,7},{7,6},{8,9},{9,8},{10,11... | collective-permute-start | bytes 393224 | tf_op jit(solution)/shard_map/ppermute | solution.py:290
  49.0 2.6 %own.1 = (f32[512,256]{1,0:T(8,128)S(1)}, s32[64,128]{1,0:T(8,128)S(1)}) custom-call(f32[256,128]{1,0:T(8,128)S(1)} %bitcast.17), custom_call_target="tpu_custom_call" | custom-call | tf_op jit(solution)/shard_map/own/pallas_call | solution.py:292
  51.6 9.0 %tile.1 = (f32[288,128]{1,0:T(8,128)}, f32[128,128]{1,0:T(8,128)S(1)}, f32[3,128]{1,0:T(4,128)}, f32[1,128]{1,0:T(1,128)}) custom-call(f32[256,128]{1,0:T(8,128)S(1)} %collective-permute-done.refs_0_, f32[512,256]{1,0:T(8,128)S(1)} %get-tuple-element.30.refs_1_, s32[64,128]{1,0:T(8,128)S(1)} %get-tuple-element.31.refs_2_, ...), custom_call_target="tpu_custom_call" | custom-call | tf_op jit(solution)/shard_map/tile/pallas_call | solution.py:297
  60.6 10.7 %all_to_all.15 = f32[32,4,128]{2,1,0:T(4,128)S(1)} all-to-all(f32[32,4,128]{2,1,0:T(4,128)S(1)} %bitcast.23), channel_id=1, replica_groups=mesh['grp'=16,'place'=16,'core'=2] {'place','core'}, dimensions={0} | all-to-all | bytes 131072 | tf_op jit(solution)/shard_map/all_to_all | solution.py:305
  71.3 0.2 ungroup.1
  71.4 0.0 copy-start.5
  71.5 14.3 %all_to_all.16.back_ref = f32[16,8,128]{2,1,0:T(8,128)S(1)} all-to-all(f32[16,8,128]{2,1,0:T(8,128)S(1)} %ungroup.1), channel_id=1, replica_groups=mesh['grp'=16,'place'=16,'core'=2] {'grp'}, dimensions={0} | all-to-all | bytes 131072 | tf_op jit(solution)/shard_map/all_to_all | solution.py:310
  85.8 1.4 %streams.1 = f32[8,128]{1,0:T(8,128)} custom-call(f32[16,8,128]{2,1,0:T(8,128)S(1)} %all_to_all.16.back_ref, f32[128,128]{1,0:T(8,128)S(1)} %get-tuple-element.38.length_ref, s32[128,128]{1,0:T(8,128)S(1)} %get-tuple-element.39.stream_ref, f32[8,128]{1,0:T(8,128)S(1)} %bitcast.25, f32[1,128]{1,0:T(1,128)S(1)} %get-tuple-element.35.refs_9_.step_ref), custom_call_target="tpu_custom_call" | custom-call | tf_op jit(solution)/shard_map/streams/pallas_call | solution.py:311
  (12 shorter events, 0.0 us)
Async XLA Ops:
  0.6 29.8 %copy-start = (f32[288,512]{1,0:T(8,128)S(1)}, f32[288,512]{1,0:T(8,128)}, u32[]{:S(2)}) copy-start(f32[288,512]{1,0:T(8,128)} %kernel_ref.1) | copy-start | bytes 1769476
  3.0 25.5 %copy-start.2 = (s32[1,512,32]{1,2,0:T(8,128)S(1)}, s32[1,512,32]{1,2,0:T(8,128)}, u32[]{:S(2)}) copy-start(s32[1,512,32]{1,2,0:T(8,128)} %param.14) | copy-start | bytes 196612
  3.0 25.5 %copy-start.6 = (s32[1,512]{1,0:T(1,128)S(1)}, s32[1,512]{1,0:T(1,128)}, u32[]{:S(2)}) copy-start(s32[1,512]{1,0:T(1,128)} %refs_2_.1) | copy-start | bytes 6148
  3.0 40.5 %all-to-all-start = ((f32[256,1,128]{2,1,0:T(1,128)}), f32[256,1,128]{2,1,0:T(1,128)S(1)}, u32[]{:S(2)}, u32[]{:S(2)}) async-start(f32[256,1,128]{2,1,0:T(1,128)} %bitcast.6), calls=%async_computation | async-start | bytes 262144 | tf_op jit(solution)/shard_map/all_to_all | solution.py:277
  28.5 0.8 copy-start.3
  29.3 0.9 %copy-start.10 = (f32[288]{0:T(512)S(1)}, f32[288]{0:T(512)}, u32[]{:S(2)}) copy-start(f32[288]{0:T(512)} %param.26) | copy-start | bytes 3460
  30.3 0.9 %copy-start.4 = (bf16[288,128]{1,0:T(8,128)(2,1)S(1)}, bf16[288,128]{1,0:T(8,128)(2,1)}, u32[]{:S(2)}) copy-start(bf16[288,128]{1,0:T(8,128)(2,1)} %signal_ref.1) | copy-start | bytes 221188
  30.3 0.9 %copy-start.8 = (s32[3,128]{1,0:T(4,128)S(1)}, s32[3,128]{1,0:T(4,128)}, u32[]{:S(2)}) copy-start(s32[3,128]{1,0:T(4,128)} %peak_ref.1) | copy-start | bytes 4612
  30.4 0.8 copy-start.7
  30.4 0.8 copy-start.9
  31.2 1.1 %copy-start.1 = (f32[288,512]{1,0:T(8,128)S(1)}, f32[288,512]{1,0:T(8,128)}, u32[]{:S(2)}) copy-start(f32[288,512]{1,0:T(8,128)} %intra_ref.1) | copy-start | bytes 1769476
  43.5 8.1 %collective-permute-start = (f32[256,128]{1,0:T(8,128)S(1)}, f32[256,128]{1,0:T(8,128)S(1)}, u32[]{:S(2)}, u32[]{:S(2)}) collective-permute-start(f32[256,128]{1,0:T(8,128)S(1)} %bitcast.16), channel_id=1, source_target_pairs={{0,1},{1,0},{2,3},{3,2},{4,5},{5,4},{6,7},{7,6},{8,9},{9,8},{10,11... | collective-permute-start | bytes 393224 | tf_op jit(solution)/shard_map/ppermute | solution.py:290
  71.4 14.3 %copy-start.5 = (f32[1024]{0:T(1024)S(1)}, f32[1024]{0:T(1024)}, u32[]{:S(2)}) copy-start(f32[1024]{0:T(1024)} %param.19) | copy-start | bytes 12292

commit v6 on v5

--- a/solution.py
+++ b/solution.py
@@ -149,8 +149,8 @@
 
 def tile_kernel(other_ref, acc_ref, own_keys_ref, backdrop_ref, parts_ref, peak_kernel_ref, extra_ref,
                 iso_ref, iso_kernel_ref, step_ref,
-                residual_ref, back_ref, new_extra_ref, new_iso_ref,
-                value_ref, keys_ref, found_ref, *, num_voxels, block, group_rows):
+                back_ref, residual_hbm, new_extra_hbm, new_iso_hbm,
+                value_ref, keys_ref, found_ref, residual_ref, new_extra_ref, new_iso_ref, sems, *, num_voxels, block, group_rows):
     core = lax.axis_index("core")
     num_bins = parts_ref.shape[2]
     rows = keys_ref.shape[1]
@@ -172,6 +172,13 @@
         new_extra_ref[k:k + 1, :] = jnp.maximum(extra_ref[k:k + 1, :] - step * grad, 0.0)
     grad = jnp.sum(iso_kernel_ref[...] * residual, axis=0, keepdims=True)
     new_iso_ref[...] = jnp.maximum(iso_ref[...] - step * grad, 0.0)
+    results = [
+        pltpu.make_async_copy(source, target, sems.at[i])
+        for i, (source, target) in enumerate((
+            (residual_ref, residual_hbm), (new_extra_ref, new_extra_hbm), (new_iso_ref, new_iso_hbm)))
+    ]
+    for copy in results:
+        copy.start()
 
     bin_ids = iota((num_bins, LANES), 0).astype(I16)
     voxel_ids = iota((num_voxels, LANES), 0)
@@ -191,6 +198,8 @@
         return carry
 
     lax.fori_loop(0, CORES, gather, 0)
+    for copy in results:
+        copy.wait()
 
 
 def ungroup_kernel(in_ref, out_ref, *, block):
@@ -231,13 +240,14 @@
 HBM = pl.BlockSpec(memory_space=pltpu.HBM)
 
 
-def call(kernel, out_shape, in_specs, name, scratch=(), limit=16):
-    multi = isinstance(out_shape, (list, tuple))
+def call(kernel, out_shape, in_specs, name, scratch=(), limit=16, out_specs=None):
+    if out_specs is None:
+        out_specs = [VMEM] * len(out_shape) if isinstance(out_shape, list) else VMEM
     return pl.pallas_call(
         kernel,
         out_shape=out_shape,
         in_specs=in_specs,
-        out_specs=[VMEM] * len(out_shape) if multi else VMEM,
+        out_specs=out_specs,
         scratch_shapes=scratch,
         compiler_params=pltpu.CompilerParams(vmem_limit_bytes=limit * 1024 * 1024),
         name=name,
@@ -294,12 +304,14 @@
         [shape((num_bins, 2 * num_voxels)), shape((own_rows, LANES), jnp.int32)], [VMEM], "own",
         scratch=[pltpu.VMEM((own_rows, LANES), F32)], limit=24,
     )(own)
-    residual, seg_back, new_extra, new_iso = call(
+    seg_back, residual, new_extra, new_iso = call(
         lambda *refs: tile_kernel(*refs, num_voxels=num_voxels, block=block, group_rows=group_rows),
-        [shape((num_dirs, num_voxels)), shape((rows, LANES)), shape(extra_weight.shape), shape((1, num_voxels))],
-        [VMEM] * 10, "tile",
+        [shape((rows, LANES)), shape((num_dirs, num_voxels)), shape(extra_weight.shape), shape((1, num_voxels))],
+        [VMEM] * 10, "tile", out_specs=[VMEM, HBM, HBM, HBM],
         scratch=[pltpu.VMEM((own_rows, LANES), F32), pltpu.VMEM((CORES, own_rows, LANES), jnp.int32),
-                 pltpu.VMEM((own_rows, LANES), F32)],
+                 pltpu.VMEM((own_rows, LANES), F32), pltpu.VMEM((num_dirs, num_voxels), F32),
+                 pltpu.VMEM(extra_weight.shape, F32), pltpu.VMEM((1, num_voxels), F32),
+                 pltpu.SemaphoreType.DMA((3,))],
         limit=32,
     )(other, acc, own_keys, backdrop, parts, peak_kernel, extra_weight, iso_row, iso_column, step_row)
     returning = lax.all_to_all(seg_back.reshape(tiles, group_rows, LANES), ("place", "core"), split_axis=0, concat_axis=0, tiled=True)

time: 87.7 us -> 87.8 us (level)
  no operation moved by 1% of the time
where the time goes in v6:
time: 87.8 us; the launch traced here: 87.3 us
  starting transfers between devices  31 us (35%)
  blocking collectives  25 us (28%)
  Pallas kernels  16.5 us (19%)
  waiting for transfers between devices  10.5 us (12%)
  local copies, waits for them, and re-layouts  2.77 us (3%)
  between operations  1.47 us (2%)
    all_to_all x1, starting transfers between devices, on_device(): lax.all_to_all(outgoing.reshape(chips, 1, LANES), ('grp', 'place'), split...  25.5 us
    all_to_all x1, blocking collectives, on_device(): lax.all_to_all(ungrouped, 'grp', split_axis=0, concat_axis=0, tiled=True)  14.3 us
    all_to_all x1, blocking collectives, on_device(): lax.all_to_all(seg_back.reshape(tiles, group_rows, LANES), ('place', 'cor...  10.7 us
    all_to_all x1, waiting for transfers between devices, on_device(): lax.all_to_all(outgoing.reshape(chips, 1, LANES), ('grp', 'place'), split...  10.5 us
    pallas_call x1, Pallas kernels, on_device(): call(lambda *refs: tile_kernel(*refs, num_voxels=num_voxels, block=block,...  9.03 us
    ppermute x1, starting transfers between devices, on_device(): other = lax.ppermute(own, 'core', [(0, 1), (1, 0)])  5.52 us
    unnamed x22, local copies, waits for them, and re-layouts  2.67 us
    pallas_call x1, Pallas kernels, on_device(): call(lambda *refs: own_kernel(*refs, num_voxels=num_voxels, block=block),...  2.56 us
  transfers between devices with their start and end apart: 2, of which 1 were waited for; matrix products, arithmetic and copies ran while one was open for 0% of the time, Pallas kernels for 4%

profile of v6, /device:TPU:1, one launch (start us, length us, event | category | flops | bytes accessed | tf_op | source)
XLA Modules:
  0.0 87.3 jit_solution(6144492186348969450)
XLA Ops:
  0.6 2.3 %prepare.1 = f32[256,128]{1,0:T(8,128)} custom-call(s32[1,32,512]{2,1,0:T(8,128)} %bitcast.18, s32[1,32,512]{2,1,0:T(8,128)} %bitcast.28, s32[1,32,512]{2,1,0:T(8,128)} %bitcast.29, f32[1,32,512]{2,1,0:T(8,128)} %bitcast.20, s32[1,512]{1,0:T(1,128)} %refs_2_.1, f32[8,128]{1,0:T(8,128)} %bitcast.24), custom_call_target="tpu_custom_call" | custom-call | tf_op jit(solution)/shard_map/prepare/pallas_call | solution.py:279
  3.0 0.0 copy-start.2
  3.0 0.0 copy-start.6
  3.0 25.5 %all-to-all-start = ((f32[256,1,128]{2,1,0:T(1,128)}), f32[256,1,128]{2,1,0:T(1,128)S(1)}, u32[]{:S(2)}, u32[]{:S(2)}) async-start(f32[256,1,128]{2,1,0:T(1,128)} %bitcast.6), calls=%async_computation | async-start | bytes 262144 | tf_op jit(solution)/shard_map/all_to_all | solution.py:287
  28.5 0.0 copy-start.3
  28.5 0.8 copy-done.3
  29.3 0.3 slots.1
  30.3 0.0 copy-start.4
  30.3 0.0 copy-start.8
  30.3 0.1 reshape.48.iso_kernel_ref.refs_8_
  30.4 0.0 copy-start.7
  30.4 0.0 copy-start.9
  30.4 0.7 copy-done.4
  31.2 1.1 %copy-done.1 = f32[288,512]{1,0:T(8,128)S(1)} copy-done((f32[288,512]{1,0:T(8,128)S(1)}, f32[288,512]{1,0:T(8,128)}, u32[]{:S(2)}) %copy-start.1) | copy-done | bytes 589848
  32.2 0.8 backdrop.1
  33.0 10.5 %all-to-all-done = f32[256,1,128]{2,1,0:T(1,128)S(1)} async-done(((f32[256,1,128]{2,1,0:T(1,128)}), f32[256,1,128]{2,1,0:T(1,128)S(1)}, u32[]{:S(2)}, u32[]{:S(2)}) %all-to-all-start) | async-done | bytes 131104 | tf_op jit(solution)/shard_map/all_to_all | solution.py:287
  43.5 5.5 %collective-permute-start = (f32[256,128]{1,0:T(8,128)S(1)}, f32[256,128]{1,0:T(8,128)S(1)}, u32[]{:S(2)}, u32[]{:S(2)}) collective-permute-start(f32[256,128]{1,0:T(8,128)S(1)} %bitcast.16), channel_id=1, source_target_pairs={{0,1},{1,0},{2,3},{3,2},{4,5},{5,4},{6,7},{7,6},{8,9},{9,8},{10,11... | collective-permute-start | bytes 393224 | tf_op jit(solution)/shard_map/ppermute | solution.py:300
  49.0 2.6 %own.1 = (f32[512,256]{1,0:T(8,128)S(1)}, s32[64,128]{1,0:T(8,128)S(1)}) custom-call(f32[256,128]{1,0:T(8,128)S(1)} %bitcast.17), custom_call_target="tpu_custom_call" | custom-call | tf_op jit(solution)/shard_map/own/pallas_call | solution.py:302
  51.6 9.0 %tile.1 = (f32[128,128]{1,0:T(8,128)S(1)}, f32[288,128]{1,0:T(8,128)}, f32[3,128]{1,0:T(4,128)}, f32[1,128]{1,0:T(1,128)}) custom-call(f32[256,128]{1,0:T(8,128)S(1)} %collective-permute-done.refs_0_, f32[512,256]{1,0:T(8,128)S(1)} %get-tuple-element.30.refs_1_, s32[64,128]{1,0:T(8,128)S(1)} %get-tuple-element.31.refs_2_, ...), custom_call_target="tpu_custom_call" | custom-call | tf_op jit(solution)/shard_map/tile/pallas_call | solution.py:307
  60.6 10.7 %all_to_all.15 = f32[32,4,128]{2,1,0:T(4,128)S(1)} all-to-all(f32[32,4,128]{2,1,0:T(4,128)S(1)} %bitcast.23), channel_id=1, replica_groups=mesh['grp'=16,'place'=16,'core'=2] {'place','core'}, dimensions={0} | all-to-all | bytes 131072 | tf_op jit(solution)/shard_map/all_to_all | solution.py:317
  71.3 0.2 ungroup.1
  71.5 0.0 copy-start.5
  71.5 14.3 %all_to_all.16.back_ref = f32[16,8,128]{2,1,0:T(8,128)S(1)} all-to-all(f32[16,8,128]{2,1,0:T(8,128)S(1)} %ungroup.1), channel_id=1, replica_groups=mesh['grp'=16,'place'=16,'core'=2] {'grp'}, dimensions={0} | all-to-all | bytes 131072 | tf_op jit(solution)/shard_map/all_to_all | solution.py:322
  85.8 1.4 %streams.1 = f32[8,128]{1,0:T(8,128)} custom-call(f32[16,8,128]{2,1,0:T(8,128)S(1)} %all_to_all.16.back_ref, f32[128,128]{1,0:T(8,128)S(1)} %get-tuple-element.38.length_ref, s32[128,128]{1,0:T(8,128)S(1)} %get-tuple-element.39.stream_ref, f32[8,128]{1,0:T(8,128)S(1)} %bitcast.25, f32[1,128]{1,0:T(1,128)S(1)} %get-tuple-element.35.refs_9_.step_ref), custom_call_target="tpu_custom_call" | custom-call | tf_op jit(solution)/shard_map/streams/pallas_call | solution.py:323
  (12 shorter events, 0.0 us)
Async XLA Ops:
  0.6 29.8 %copy-start = (f32[288,512]{1,0:T(8,128)S(1)}, f32[288,512]{1,0:T(8,128)}, u32[]{:S(2)}) copy-start(f32[288,512]{1,0:T(8,128)} %kernel_ref.1) | copy-start | bytes 1769476
  3.0 25.5 %copy-start.2 = (s32[1,512,32]{1,2,0:T(8,128)S(1)}, s32[1,512,32]{1,2,0:T(8,128)}, u32[]{:S(2)}) copy-start(s32[1,512,32]{1,2,0:T(8,128)} %param.14) | copy-start | bytes 196612
  3.0 25.5 %copy-start.6 = (s32[1,512]{1,0:T(1,128)S(1)}, s32[1,512]{1,0:T(1,128)}, u32[]{:S(2)}) copy-start(s32[1,512]{1,0:T(1,128)} %refs_2_.1) | copy-start | bytes 6148
  3.0 40.5 %all-to-all-start = ((f32[256,1,128]{2,1,0:T(1,128)}), f32[256,1,128]{2,1,0:T(1,128)S(1)}, u32[]{:S(2)}, u32[]{:S(2)}) async-start(f32[256,1,128]{2,1,0:T(1,128)} %bitcast.6), calls=%async_computation | async-start | bytes 262144 | tf_op jit(solution)/shard_map/all_to_all | solution.py:287
  28.5 0.8 copy-start.3
  29.3 0.9 %copy-start.10 = (f32[288]{0:T(512)S(1)}, f32[288]{0:T(512)}, u32[]{:S(2)}) copy-start(f32[288]{0:T(512)} %param.26) | copy-start | bytes 3460
  30.3 0.9 %copy-start.4 = (bf16[288,128]{1,0:T(8,128)(2,1)S(1)}, bf16[288,128]{1,0:T(8,128)(2,1)}, u32[]{:S(2)}) copy-start(bf16[288,128]{1,0:T(8,128)(2,1)} %signal_ref.1) | copy-start | bytes 221188
  30.3 0.9 %copy-start.8 = (s32[3,128]{1,0:T(4,128)S(1)}, s32[3,128]{1,0:T(4,128)}, u32[]{:S(2)}) copy-start(s32[3,128]{1,0:T(4,128)} %peak_ref.1) | copy-start | bytes 4612
  30.4 0.8 copy-start.7
  30.4 0.8 copy-start.9
  31.2 1.1 %copy-start.1 = (f32[288,512]{1,0:T(8,128)S(1)}, f32[288,512]{1,0:T(8,128)}, u32[]{:S(2)}) copy-start(f32[288,512]{1,0:T(8,128)} %intra_ref.1) | copy-start | bytes 1769476
  43.5 8.1 %collective-permute-start = (f32[256,128]{1,0:T(8,128)S(1)}, f32[256,128]{1,0:T(8,128)S(1)}, u32[]{:S(2)}, u32[]{:S(2)}) collective-permute-start(f32[256,128]{1,0:T(8,128)S(1)} %bitcast.16), channel_id=1, source_target_pairs={{0,1},{1,0},{2,3},{3,2},{4,5},{5,4},{6,7},{7,6},{8,9},{9,8},{10,11... | collective-permute-start | bytes 393224 | tf_op jit(solution)/shard_map/ppermute | solution.py:300
  71.5 14.4 %copy-start.5 = (f32[1024]{0:T(1024)S(1)}, f32[1024]{0:T(1024)}, u32[]{:S(2)}) copy-start(f32[1024]{0:T(1024)} %param.19) | copy-start | bytes 12292
